TPU v7x, 32 devices: a whole 2x2x4 slice. The times are simulated.
32 devices in a mesh: ctx: 4 (over y, x), dp: 8 (over z, core).
Axes of the slice: x: 2, y: 2, z: 4, core: 2. Of those that a mesh axis runs over, the one named last changes fastest.
Arguments:
- queries: bfloat16 [8, 512, 2048], P('dp', 'ctx'), may hold values from -64 to 64
- keys: bfloat16 [8, 512, 1024], P('dp', 'ctx'), may hold values from -64 to 64
- values: bfloat16 [8, 512, 1024], P('dp', 'ctx'), may hold values from -6 to 6
- grad_out: bfloat16 [8, 512, 2048], P('dp', 'ctx'), may hold values from -40 to 40
- query_gain: float32 [128], replicated, may hold values from 0.5 to 6.5
- key_gain: float32 [128], replicated, may hold values from 0.5 to 6.5
- doc_lengths: int32 [8, 4], P('dp'), may hold values from 1 to 256, 512 in all within a row
Outputs:
- query_grad: bfloat16 [8, 512, 2048], P('dp', 'ctx')
- key_gradient: bfloat16 [8, 512, 1024], P('dp', 'ctx')
- value_gradient: bfloat16 [8, 512, 1024], P('dp', 'ctx')
- query_gain_grad: float32 [128], replicated
- key_gain_grad: float32 [128], replicated
Inputs may be any that keep to these rules, and one draw needn't show every extreme that they name: `doc_lengths`: each row sums to 512.
All inputs are finite; a program needn't handle non-finite values.
Results may differ from a plain program's by a relative error of at most 0.024.
The roundings to bfloat16 on the way count: a program that leaves them out, or rounds other values in their place, can miss the bound.
Values may be sent and summed in bfloat16 or wider, within the bound.
No kernel may reach another device: no remote copies, remote signals or barrier semaphores. Data moves between devices by JAX's collectives and lax.ppermute only.
A program may use at most 64 MiB of HBM per device.

v0:
```python
import jax
import jax.numpy as jnp
from jax import lax
from jax.experimental import pallas as pl
from jax.experimental.pallas import tpu as pltpu
from jax.sharding import PartitionSpec as P


QUERY_HEADS = 16
KEY_VALUE_HEADS = 8
HEAD_SIZE = 128
WINDOW_SIZE = 256
GROUP = QUERY_HEADS // KEY_VALUE_HEADS

norm_epsilon = 1e-06
score_scale = 168.0 ** (-0.5)
MASKED = -1e30
LOG2E = 1.4426950408889634
VMEM_LIMIT = 16 << 20


F32 = jnp.float32
BF16 = jnp.bfloat16


def dot(a, b, ca, cb):
    return lax.dot_general(a, b, (((ca,), (cb,)), ((), ())), preferred_element_type=F32)


def inverse_rms(x):
    return lax.rsqrt(jnp.mean(x * x, axis=-1, keepdims=True) + norm_epsilon)


def document_of(lengths_ref, positions):
    index = jnp.zeros(positions.shape, jnp.int32)
    end = jnp.int32(0)
    for doc in range(lengths_ref.shape[1]):
        end = end + lengths_ref[0, doc]
        index = index + (positions >= end).astype(jnp.int32)
    return index


def mask_bias(lengths_ref, first, keys, rows):
    key_pos = first - WINDOW_SIZE + lax.broadcasted_iota(jnp.int32, (keys, 1), 0)
    query_pos = first + lax.broadcasted_iota(jnp.int32, (1, rows), 1)
    key_doc = jnp.where(key_pos >= 0, document_of(lengths_ref, key_pos), -1)
    query_doc = document_of(lengths_ref, query_pos)
    gap = query_pos - key_pos
    allowed = (key_doc == query_doc) & (gap >= 0) & (gap < WINDOW_SIZE)
    return jnp.where(allowed, 0.0, MASKED).astype(F32)


def stacked(ref, u):
    parts = [ref[:, (u * GROUP + i) * HEAD_SIZE:(u * GROUP + i + 1) * HEAD_SIZE] for i in range(GROUP)]
    return jnp.concatenate(parts, axis=0)


def columns(u):
    return slice(u * HEAD_SIZE, (u + 1) * HEAD_SIZE)


def prepare_kernel(first_ref, lengths_ref, q_ref, k_ref, v_ref, go_ref, qg_ref, kg_ref,
                   q2_ref, qn_ref, kn_ref, s_ref, dp_ref, go2_ref, got_ref, v0_ref, bias_ref):
    rows = q_ref.shape[0]

    bias = mask_bias(lengths_ref, first_ref[0], WINDOW_SIZE + rows, rows)
    bias_ref[...] = bias[:WINDOW_SIZE]
    bias = jnp.concatenate([bias[WINDOW_SIZE:]] * GROUP, axis=1)
    for u in range(KEY_VALUE_HEADS):
        raw = stacked(q_ref, u)
        q2_ref[u] = raw
        q = raw.astype(F32)
        go = stacked(go_ref, u)
        go2_ref[u] = go
        v0_ref[:, columns(u)] = v_ref[:, columns(u)]
        qn = (q * inverse_rms(q) * qg_ref[...]).astype(BF16)
        k = k_ref[:, columns(u)].astype(F32)
        kn = (k * inverse_rms(k) * kg_ref[...]).astype(BF16)
        qn_ref[u] = qn
        kn_ref[:, columns(u)] = kn
        s_ref[u] = dot(kn, qn, 1, 1) * (score_scale * LOG2E) + bias
        dp_ref[u] = dot(v_ref[:, columns(u)], go, 1, 1)
        got_ref[u] = jnp.transpose(go)


def weigh_kernel(qn_ref, kn0_ref, s_ref, bias_ref, k1_ref, k2_ref, go_ref, kg_ref, kn_ref, p_ref, g1v_ref, g2v_ref):
    rows = kn0_ref.shape[0]
    bias = jnp.concatenate([bias_ref[...]] * GROUP, axis=1)
    kn_ref[WINDOW_SIZE:, :] = kn0_ref[...]
    for u in range(KEY_VALUE_HEADS):
        k = jnp.concatenate([k2_ref[:, columns(u)], k1_ref[:, columns(u)]], axis=0).astype(F32)
        kn = (k * inverse_rms(k) * kg_ref[...]).astype(BF16)
        kn_ref[:WINDOW_SIZE, columns(u)] = kn
        s = dot(kn, qn_ref[u], 1, 1) * (score_scale * LOG2E) + bias
        s0 = s_ref[u]
        top = jnp.maximum(jnp.max(s, axis=0, keepdims=True), jnp.max(s0, axis=0, keepdims=True))
        e, e0 = jnp.exp2(s - top), jnp.exp2(s0 - top)
        inv = 1.0 / (jnp.sum(e, axis=0, keepdims=True) + jnp.sum(e0, axis=0, keepdims=True))
        p = e * inv
        p_ref[u, :WINDOW_SIZE] = p
        p_ref[u, WINDOW_SIZE:] = e0 * inv
        g = dot(p.astype(BF16), go_ref[u], 1, 0).astype(BF16)
        g2v_ref[:, columns(u)] = g[:rows]
        g1v_ref[:, columns(u)] = g[rows:]


def score_kernel(p_ref, v0_ref, v1_ref, v2_ref, go_ref, got_ref, dp_ref, q_ref, qn_ref, kn_ref, qg_ref, kg_ref,
                 g1k_ref, g2k_ref, dq_ref, dk_ref, dv_ref, gains_ref):
    rows = v0_ref.shape[0]
    q_part = jnp.zeros((1, HEAD_SIZE), F32)
    k_part = jnp.zeros((1, HEAD_SIZE), F32)
    for u in range(KEY_VALUE_HEADS):
        v = jnp.concatenate([v2_ref[:, columns(u)], v1_ref[:, columns(u)]], axis=0)
        go, qn = go_ref[u], qn_ref[u]
        p, p0 = p_ref[u, :WINDOW_SIZE], p_ref[u, WINDOW_SIZE:]
        p0_low = p0.astype(BF16)
        attended = dot(v, p.astype(BF16), 0, 0) + dot(v0_ref[:, columns(u)], p0_low, 0, 0)
        attended = attended.astype(BF16).astype(F32)
        delta = jnp.sum(got_ref[u].astype(F32) * attended, axis=0, keepdims=True)
        ds = (p * (dot(v, go, 1, 1) - delta)).astype(BF16)
        ds0 = (p0 * (dp_ref[u] - delta)).astype(BF16)
        g = (dot(ds, qn, 1, 0) * score_scale).astype(BF16)
        g2k_ref[:, columns(u)] = g[:rows]
        g1k_ref[:, columns(u)] = g[rows:]
        kn = kn_ref[:, columns(u)]
        dqn = dot(jnp.concatenate([ds, ds0], axis=0), kn, 0, 0) * score_scale
        dk_ref[:, columns(u)] = dot(ds0, qn, 1, 0) * score_scale
        dv_ref[:, columns(u)] = dot(p0_low, go, 1, 0)
        q = q_ref[u].astype(F32)
        q_inv = inverse_rms(q)
        q_hat = q * q_inv
        q_part = q_part + jnp.sum(dqn * q_hat, axis=0, keepdims=True)
        k_part = k_part + jnp.sum(dqn * qn.astype(F32), axis=0, keepdims=True)
        t = dqn * qg_ref[...]
        dq = (q_inv * (t - q_hat * jnp.mean(t * q_hat, axis=-1, keepdims=True))).astype(BF16)
        for i in range(GROUP):
            dq_ref[:, columns(u * GROUP + i)] = dq[i * rows:(i + 1) * rows]
    gains_ref[...] = jnp.zeros_like(gains_ref)
    gains_ref[0:1, :] = q_part
    gains_ref[1:2, :] = k_part / kg_ref[...]


def value_kernel(dv_ref, a_ref, b_ref, out_ref):
    out_ref[...] = (dv_ref[...] + a_ref[...].astype(F32) + b_ref[...].astype(F32)).astype(BF16)


def key_kernel(odd_ref, k_ref, dk_ref, a_ref, b_ref, kg_ref, out_ref):
    keep = (odd_ref[0] == 0).astype(F32)
    for h in range(k_ref.shape[1] // HEAD_SIZE):
        total = dk_ref[:, columns(h)] + a_ref[:, columns(h)].astype(F32) * keep + b_ref[:, columns(h)].astype(F32)
        k = k_ref[:, columns(h)].astype(F32)
        inv = inverse_rms(k)
        k_hat = k * inv
        t = total * kg_ref[...]
        out_ref[:, columns(h)] = (inv * (t - k_hat * jnp.mean(t * k_hat, axis=-1, keepdims=True))).astype(BF16)


def call(kernel, outs, args, scalars=()):
    vmem = pl.BlockSpec(memory_space=pltpu.VMEM)
    return pl.pallas_call(
        kernel,
        in_specs=[pl.BlockSpec(memory_space=pltpu.SMEM)] * len(scalars) + [vmem] * len(args),
        out_specs=[vmem] * len(outs),
        out_shape=outs,
        compiler_params=pltpu.CompilerParams(vmem_limit_bytes=VMEM_LIMIT),
    )(*scalars, *args)


def near(*arrays):
    return tuple(pltpu.with_memory_space_constraint(array, pltpu.VMEM) for array in arrays)


def far(*arrays):
    return tuple(pltpu.with_memory_space_constraint(array, pltpu.HBM) for array in arrays)


def sum_over(x, axis):
    count, stride = lax.axis_size(axis), 1
    while stride < count:
        rest = count // stride
        radix = next(f for f in range(2, rest + 1) if rest % f == 0)

        def moved(turn):
            pairs = []
            for source in range(count):
                digit = source // stride % radix
                pairs.append((source, source + ((digit + turn) % radix - digit) * stride))
            return lax.ppermute(x, axis, pairs)

        parts = [moved(turn) for turn in range(1, radix)]
        x = x + sum(parts)
        stride = stride * radix
    return x


def per_device(queries, keys, values, grad_out, query_gain, key_gain, doc_lengths):
    rows = queries.shape[1]
    count = lax.axis_size("ctx")
    assert rows * 2 == WINDOW_SIZE and count % 2 == 0
    here = lax.axis_index("ctx")
    odd = lax.rem(here, 2)
    first = (here * rows).astype(jnp.int32)
    q, k, v, go = queries[0], keys[0], values[0], grad_out[0]
    q_gain, k_gain = query_gain[None], key_gain[None]

    ahead = [(i, (i + 2) % count) for i in range(count)]
    behind = [(i, (i - 2) % count) for i in range(count)]
    follow = [(i, (i + 1) % count) for i in range(count)]
    lead = [(i, (i - 1) % count) for i in range(count)]
    swap = [(i, i ^ 1) for i in range(count)]

    pair, keys, heads = GROUP * rows, WINDOW_SIZE + rows, KEY_VALUE_HEADS
    flat = (rows, heads * HEAD_SIZE)
    tie = lax.optimization_barrier

    held, away = pltpu.VMEM, jax.ShapeDtypeStruct
    k2 = lax.ppermute(k, "ctx", ahead)
    q2, qn, kn0, s0, dp0, go2, go_t, v0, bias = call(
        prepare_kernel,
        [
            held((heads, pair, HEAD_SIZE), BF16), held((heads, pair, HEAD_SIZE), BF16), held(flat, BF16),
            held((heads, rows, pair), F32), held((heads, rows, pair), F32),
            held((heads, pair, HEAD_SIZE), BF16), held((heads, HEAD_SIZE, pair), BF16),
            held(flat, BF16), held((WINDOW_SIZE, rows), F32),
        ],
        far(q, k, v, go, q_gain, k_gain), (first[None],) + far(doc_lengths),
    )
    turned = jnp.where(odd == 1, k2, k)
    k1 = lax.ppermute(turned, "ctx", swap)
    late_v, _ = tie((v, turned))
    v2 = lax.ppermute(late_v, "ctx", ahead)
    v1 = lax.ppermute(late_v, "ctx", follow)

    kn, p, g1v, g2v = call(
        weigh_kernel,
        [
            held((keys, heads * HEAD_SIZE), BF16), held((heads, keys, pair), F32),
            held(flat, BF16), held(flat, BF16),
        ],
        near(qn, kn0, s0, bias, k1, k2, go2) + far(k_gain),
    )
    av = lax.ppermute(g1v, "ctx", lead)
    bv = lax.ppermute(g2v, "ctx", behind)

    g1k, g2k, dq, dk_own, dv_own, gains = call(
        score_kernel,
        [
            held(flat, BF16), held(flat, BF16), away(q.shape, BF16),
            held(flat, F32), held(flat, F32), held((8, HEAD_SIZE), F32),
        ],
        near(p, v0, v1, v2, go2, go_t, dp0, q2, qn, kn) + far(q_gain, k_gain),
    )
    ak = lax.ppermute(g1k, "ctx", swap)
    keep = (odd == 1).astype(F32)
    joined = (g2k.astype(F32) + ak.astype(F32) * keep).astype(BF16)
    bk = lax.ppermute(joined, "ctx", behind)
    gains = sum_over(sum_over(gains, "dp"), "ctx")

    dv = call(value_kernel, [away(flat, BF16)], near(dv_own, av, bv))[0]
    dk = call(
        key_kernel, [away(flat, BF16)],
        far(k) + near(dk_own, ak, bk) + far(k_gain), (odd.astype(jnp.int32)[None],),
    )[0]
    return (dq[None], dk[None], dv[None], gains[0], gains[1])


def solution(mesh):
    in_specs = (
        P("dp", "ctx", None),
        P("dp", "ctx", None),
        P("dp", "ctx", None),
        P("dp", "ctx", None),
        P(),
        P(),
        P("dp", None),
    )
    out_specs = (P("dp", "ctx", None), P("dp", "ctx", None), P("dp", "ctx", None), P(), P())
    return jax.shard_map(
        per_device, mesh=mesh, in_specs=in_specs, out_specs=out_specs, check_vma=False
    )
```

profile of v0, /device:TPU:0, one launch (start us, length us, event | category | flops | bytes accessed | tf_op | source)
XLA Modules:
  0.0 60.6 jit_solution(855050451254366617)
XLA Ops:
  0.6 3.1 %collective-permute-start = (bf16[128,1024]{1,0:T(8,128)(2,1)}, bf16[128,1024]{1,0:T(8,128)(2,1)S(1)}, u32[]{:S(2)}, u32[]{:S(2)}) collective-permute-start(bf16[128,1024]{1,0:T(8,128)(2,1)} %bitcast.16), channel_id=1, source_target_pairs={{0,16},{8,24},{16,0},{24,8},{1,17},{9,25},{17,1},{25,9},{2,18},{10... | collective-permute-start | bytes 786440 | tf_op jit(solution)/shard_map/ppermute | solution.py:217
  3.7 6.5 %collective-permute-done.k2_ref = bf16[128,1024]{1,0:T(8,128)(2,1)S(1)} collective-permute-done((bf16[128,1024]{1,0:T(8,128)(2,1)}, bf16[128,1024]{1,0:T(8,128)(2,1)S(1)}, u32[]{:S(2)}, u32[]{:S(2)}) %collective-permute-start) | collective-permute-done | bytes 262176 | tf_op jit(solution)/shard_map/ppermute | solution.py:217
  10.2 1.0 %broadcast_select_fusion = bf16[128,1024]{1,0:T(8,128)(2,1)S(1)} fusion(bf16[128,1024]{1,0:T(8,128)(2,1)S(1)} %collective-permute-done.k2_ref, pred[]{:T(512)S(6)} %eq.4, bf16[1,128,1024]{2,1,0:T(8,128)(2,1)} %param.8), kind=kLoop, calls=%fused_computation.1 | loop fusion | flops 131072 | bytes 786433 | tf_op jit(solution)/shard_map/jit(_where)/select_n | solution.py:228
  11.2 1.8 %collective-permute-start.1 = (bf16[128,1024]{1,0:T(8,128)(2,1)S(1)}, bf16[128,1024]{1,0:T(8,128)(2,1)S(1)}, u32[]{:S(2)}, u32[]{:S(2)}) collective-permute-start(bf16[128,1024]{1,0:T(8,128)(2,1)S(1)} %broadcast_select_fusion), channel_id=1, source_target_pairs={{0,8},{8,0},{16,24},{24,16},{1,9},{9,1},{17,25},{25,17},{2,10},{10... | collective-permute-start | bytes 786440 | tf_op jit(solution)/shard_map/ppermute | solution.py:229
  13.0 1.5 %collective-permute-start.3 = (bf16[128,1024]{1,0:T(8,128)(2,1)}, bf16[128,1024]{1,0:T(8,128)(2,1)S(1)}, u32[]{:S(2)}, u32[]{:S(2)}) collective-permute-start(bf16[128,1024]{1,0:T(8,128)(2,1)} %bitcast.22), channel_id=1, source_target_pairs={{0,16},{8,24},{16,0},{24,8},{1,17},{9,25},{17,1},{25,9},{2,18},{10... | collective-permute-start | bytes 786440 | tf_op jit(solution)/shard_map/ppermute | solution.py:231
  15.0 2.3 %shard_map.110 = (bf16[8,256,128]{2,1,0:T(8,128)(2,1)S(1)}, bf16[8,256,128]{2,1,0:T(8,128)(2,1)S(1)}, bf16[128,1024]{1,0:T(8,128)(2,1)S(1)}, f32[8,128,256]{2,1,...) custom-call(s32[1]{0:T(128)} %bitcast.first_ref, ...), custom_call_target="tpu_custom_call" | custom-call | tf_op jit(solution)/shard_map/pallas_call | solution.py:160
  17.4 3.1 %collective-permute-done.1.k1_ref = bf16[128,1024]{1,0:T(8,128)(2,1)S(1)} collective-permute-done((bf16[128,1024]{1,0:T(8,128)(2,1)S(1)}, bf16[128,1024]{1,0:T(8,128)(2,1)S(1)}, u32[]{:S(2)}, u32[]{:S(2)}) %collective-permute-start.1) | collective-permute-done | bytes 262176 | tf_op jit(solution)/shard_map/ppermute | solution.py:229
  20.4 2.5 %shard_map.111 = (bf16[384,1024]{1,0:T(8,128)(2,1)S(1)}, f32[8,384,256]{2,1,0:T(8,128)S(1)}, bf16[128,1024]{1,0:T(8,128)(2,1)S(1)}, bf16[128,1024]{1,0:T(8,128)(2,1)S(1)}) custom-call(bf16[8,256,128]{2,1,0:T(8,128)(2,1)S(1)} %get-tuple-element.25.qn_ref, bf16[128,1024]{1,0:T(8,128)(2,1)S(1)} %get-tuple-element.26.kn0_ref, ...), custom_call_target="tpu_custom_call" | custom-call | tf_op jit(solution)/shard_map/pallas_call | solution.py:160
  23.0 2.7 %collective-permute-done.3.v2_ref = bf16[128,1024]{1,0:T(8,128)(2,1)S(1)} collective-permute-done((bf16[128,1024]{1,0:T(8,128)(2,1)}, bf16[128,1024]{1,0:T(8,128)(2,1)S(1)}, u32[]{:S(2)}, u32[]{:S(2)}) %collective-permute-start.3) | collective-permute-done | bytes 262176 | tf_op jit(solution)/shard_map/ppermute | solution.py:231
  25.7 5.1 %shard_map.112 = (bf16[128,1024]{1,0:T(8,128)(2,1)S(1)}, bf16[128,1024]{1,0:T(8,128)(2,1)S(1)}, bf16[128,2048]{1,0:T(8,128)(2,1)}, f32[128,1024]{1,0:T(8,128)S(1...) custom-call(f32[8,384,256]{2,1,0:T(8,128)S(1)} %get-tuple-element.30.p_ref, ...), custom_call_target="tpu_custom_call" | custom-call | tf_op jit(solution)/shard_map/pallas_call | solution.py:160
  30.9 2.9 %collective-permute-start.6 = (bf16[128,1024]{1,0:T(8,128)(2,1)S(1)}, bf16[128,1024]{1,0:T(8,128)(2,1)S(1)}, u32[]{:S(2)}, u32[]{:S(2)}) collective-permute-start(bf16[128,1024]{1,0:T(8,128)(2,1)S(1)} %get-tuple-element.42), channel_id=1, source_target_pairs={{0,24},{8,0},{16,8},{24,16},{1,25},{9,1},{17,9},{25,17},{2,26},{10... | collective-permute-start | bytes 786440 | tf_op jit(solution)/shard_map/ppermute | solution.py:242
  34.3 5.2 %collective-permute-done.4.a_ref = bf16[128,1024]{1,0:T(8,128)(2,1)S(1)} collective-permute-done((bf16[128,1024]{1,0:T(8,128)(2,1)S(1)}, bf16[128,1024]{1,0:T(8,128)(2,1)S(1)}, u32[]{:S(2)}, u32[]{:S(2)}) %collective-permute-start.4) | collective-permute-done | bytes 262176 | tf_op jit(solution)/shard_map/ppermute | solution.py:253
  39.6 0.9 %collective-permute-start.5 = (bf16[128,1024]{1,0:T(8,128)(2,1)S(1)}, bf16[128,1024]{1,0:T(8,128)(2,1)S(1)}, u32[]{:S(2)}, u32[]{:S(2)}) collective-permute-start(bf16[128,1024]{1,0:T(8,128)(2,1)S(1)} %add_convert_fusion), channel_id=1, source_target_pairs={{0,16},{8,24},{16,0},{24,8},{1,17},{9,25},{17,1},{25,9},{2,18},{10... | collective-permute-start | bytes 786440 | tf_op jit(solution)/shard_map/ppermute | solution.py:256
  40.5 1.2 %collective-permute-done.8 = f32[8,128]{1,0:T(8,128)S(1)} collective-permute-done((f32[8,128]{1,0:T(8,128)S(1)}, f32[8,128]{1,0:T(8,128)S(1)}, u32[]{:S(2)}, u32[]{:S(2)}) %collective-permute-start.8) | collective-permute-done | bytes 4128 | tf_op jit(solution)/shard_map/ppermute | solution.py:188
  41.7 1.2 %collective-permute-start.9 = (f32[8,128]{1,0:T(8,128)S(1)}, f32[8,128]{1,0:T(8,128)S(1)}, u32[]{:S(2)}, u32[]{:S(2)}) collective-permute-start(f32[8,128]{1,0:T(8,128)S(1)} %add.19), channel_id=1, source_target_pairs={{0,2},{1,3},{2,0},{3,1},{4,6},{5,7},{6,4},{7,5},{8,10},{9,11},{10,... | collective-permute-start | bytes 12296 | tf_op jit(solution)/shard_map/ppermute | solution.py:188
  42.9 2.4 %collective-permute-done.9 = f32[8,128]{1,0:T(8,128)S(1)} collective-permute-done((f32[8,128]{1,0:T(8,128)S(1)}, f32[8,128]{1,0:T(8,128)S(1)}, u32[]{:S(2)}, u32[]{:S(2)}) %collective-permute-start.9) | collective-permute-done | bytes 4128 | tf_op jit(solution)/shard_map/ppermute | solution.py:188
  45.3 2.2 %collective-permute-start.10 = (f32[8,128]{1,0:T(8,128)S(1)}, f32[8,128]{1,0:T(8,128)S(1)}, u32[]{:S(2)}, u32[]{:S(2)}) collective-permute-start(f32[8,128]{1,0:T(8,128)S(1)} %add.20), channel_id=1, source_target_pairs={{0,4},{1,5},{2,6},{3,7},{4,0},{5,1},{6,2},{7,3},{8,12},{9,13},{10,... | collective-permute-start | bytes 12296 | tf_op jit(solution)/shard_map/ppermute | solution.py:188
  47.6 2.3 %collective-permute-done.10 = f32[8,128]{1,0:T(8,128)S(1)} collective-permute-done((f32[8,128]{1,0:T(8,128)S(1)}, f32[8,128]{1,0:T(8,128)S(1)}, u32[]{:S(2)}, u32[]{:S(2)}) %collective-permute-start.10) | collective-permute-done | bytes 4128 | tf_op jit(solution)/shard_map/ppermute | solution.py:188
  49.8 1.2 %collective-permute-start.11 = (f32[8,128]{1,0:T(8,128)S(1)}, f32[8,128]{1,0:T(8,128)S(1)}, u32[]{:S(2)}, u32[]{:S(2)}) collective-permute-start(f32[8,128]{1,0:T(8,128)S(1)} %add.21), channel_id=1, source_target_pairs={{0,8},{8,0},{16,24},{24,16},{1,9},{9,1},{17,25},{25,17},{2,10},{10... | collective-permute-start | bytes 12296 | tf_op jit(solution)/shard_map/ppermute | solution.py:188
  51.0 2.4 %collective-permute-done.11 = f32[8,128]{1,0:T(8,128)S(1)} collective-permute-done((f32[8,128]{1,0:T(8,128)S(1)}, f32[8,128]{1,0:T(8,128)S(1)}, u32[]{:S(2)}, u32[]{:S(2)}) %collective-permute-start.11) | collective-permute-done | bytes 4128 | tf_op jit(solution)/shard_map/ppermute | solution.py:188
  53.4 1.2 %collective-permute-start.12 = (f32[8,128]{1,0:T(8,128)S(1)}, f32[8,128]{1,0:T(8,128)S(1)}, u32[]{:S(2)}, u32[]{:S(2)}) collective-permute-start(f32[8,128]{1,0:T(8,128)S(1)} %add.22), channel_id=1, source_target_pairs={{0,16},{8,24},{16,0},{24,8},{1,17},{9,25},{17,1},{25,9},{2,18},{10... | collective-permute-start | bytes 12296 | tf_op jit(solution)/shard_map/ppermute | solution.py:188
  54.6 2.4 %collective-permute-done.12 = f32[8,128]{1,0:T(8,128)S(1)} collective-permute-done((f32[8,128]{1,0:T(8,128)S(1)}, f32[8,128]{1,0:T(8,128)S(1)}, u32[]{:S(2)}, u32[]{:S(2)}) %collective-permute-start.12) | collective-permute-done | bytes 4128 | tf_op jit(solution)/shard_map/ppermute | solution.py:188
  57.6 0.8 %shard_map.114 = bf16[128,1024]{1,0:T(8,128)(2,1)} custom-call(f32[128,1024]{1,0:T(8,128)S(1)} %get-tuple-element.41.dv_ref, bf16[128,1024]{1,0:T(8,128)(2,1)S(1)} %collective-permute-done.6.a_ref, bf16[128,1024]{1,0:T(8,128)(2,1)S(1)} %collective-permute-done.7.b_ref), custom_call_target="tpu_custom_call" | custom-call | tf_op jit(solution)/shard_map/pallas_call | solution.py:160
  58.4 2.2 %shard_map.113 = bf16[128,1024]{1,0:T(8,128)(2,1)} custom-call(s32[1]{0:T(128)} %bitcast.8.odd_ref, bf16[128,1024]{1,0:T(8,128)(2,1)} %bitcast.18, f32[128,1024]{1,0:T(8,128)S(1)} %get-tuple-element.38.dk_ref, bf16[128,1024]{1,0:T(8,128)(2,1)S(1)} %collective-permute-done.4.a_ref, bf16[128,1024]{1,0:T(8,128)(2,1)S(1)} %collective-permute-done.5.b_ref, ...), custom_call_target="tpu_custom_call" | custom-call | tf_op jit(solution)/shard_map/pallas_call | solution.py:160
  (15 shorter events, 1.7 us)
Async XLA Ops:
  0.6 9.6 %collective-permute-start = (bf16[128,1024]{1,0:T(8,128)(2,1)}, bf16[128,1024]{1,0:T(8,128)(2,1)S(1)}, u32[]{:S(2)}, u32[]{:S(2)}) collective-permute-start(bf16[128,1024]{1,0:T(8,128)(2,1)} %bitcast.16), channel_id=1, source_target_pairs={{0,16},{8,24},{16,0},{24,8},{1,17},{9,25},{17,1},{25,9},{2,18},{10... | collective-permute-start | bytes 786440 | tf_op jit(solution)/shard_map/ppermute | solution.py:217
  11.2 9.2 %collective-permute-start.1 = (bf16[128,1024]{1,0:T(8,128)(2,1)S(1)}, bf16[128,1024]{1,0:T(8,128)(2,1)S(1)}, u32[]{:S(2)}, u32[]{:S(2)}) collective-permute-start(bf16[128,1024]{1,0:T(8,128)(2,1)S(1)} %broadcast_select_fusion), channel_id=1, source_target_pairs={{0,8},{8,0},{16,24},{24,16},{1,9},{9,1},{17,25},{25,17},{2,10},{10... | collective-permute-start | bytes 786440 | tf_op jit(solution)/shard_map/ppermute | solution.py:229
  13.0 12.7 %collective-permute-start.3 = (bf16[128,1024]{1,0:T(8,128)(2,1)}, bf16[128,1024]{1,0:T(8,128)(2,1)S(1)}, u32[]{:S(2)}, u32[]{:S(2)}) collective-permute-start(bf16[128,1024]{1,0:T(8,128)(2,1)} %bitcast.22), channel_id=1, source_target_pairs={{0,16},{8,24},{16,0},{24,8},{1,17},{9,25},{17,1},{25,9},{2,18},{10... | collective-permute-start | bytes 786440 | tf_op jit(solution)/shard_map/ppermute | solution.py:231
  14.5 11.2 %collective-permute-start.2 = (bf16[128,1024]{1,0:T(8,128)(2,1)}, bf16[128,1024]{1,0:T(8,128)(2,1)S(1)}, u32[]{:S(2)}, u32[]{:S(2)}) collective-permute-start(bf16[128,1024]{1,0:T(8,128)(2,1)} %bitcast.23), channel_id=1, source_target_pairs={{0,8},{8,16},{16,24},{24,0},{1,9},{9,17},{17,25},{25,1},{2,10},{10... | collective-permute-start | bytes 786440 | tf_op jit(solution)/shard_map/ppermute | solution.py:232
  30.8 8.7 %collective-permute-start.4 = (bf16[128,1024]{1,0:T(8,128)(2,1)S(1)}, bf16[128,1024]{1,0:T(8,128)(2,1)S(1)}, u32[]{:S(2)}, u32[]{:S(2)}) collective-permute-start(bf16[128,1024]{1,0:T(8,128)(2,1)S(1)} %get-tuple-element.39), channel_id=1, source_target_pairs={{0,8},{8,0},{16,24},{24,16},{1,9},{9,1},{17,25},{25,17},{2,10},{10... | collective-permute-start | bytes 786440 | tf_op jit(solution)/shard_map/ppermute | solution.py:253
  30.9 26.7 %collective-permute-start.6 = (bf16[128,1024]{1,0:T(8,128)(2,1)S(1)}, bf16[128,1024]{1,0:T(8,128)(2,1)S(1)}, u32[]{:S(2)}, u32[]{:S(2)}) collective-permute-start(bf16[128,1024]{1,0:T(8,128)(2,1)S(1)} %get-tuple-element.42), channel_id=1, source_target_pairs={{0,24},{8,0},{16,8},{24,16},{1,25},{9,1},{17,9},{25,17},{2,26},{10... | collective-permute-start | bytes 786440 | tf_op jit(solution)/shard_map/ppermute | solution.py:242
  33.8 23.8 %collective-permute-start.7 = (bf16[128,1024]{1,0:T(8,128)(2,1)S(1)}, bf16[128,1024]{1,0:T(8,128)(2,1)S(1)}, u32[]{:S(2)}, u32[]{:S(2)}) collective-permute-start(bf16[128,1024]{1,0:T(8,128)(2,1)S(1)} %get-tuple-element.43), channel_id=1, source_target_pairs={{0,16},{8,24},{16,0},{24,8},{1,17},{9,25},{17,1},{25,9},{2,18},{10... | collective-permute-start | bytes 786440 | tf_op jit(solution)/shard_map/ppermute | solution.py:243
  39.6 18.8 %collective-permute-start.5 = (bf16[128,1024]{1,0:T(8,128)(2,1)S(1)}, bf16[128,1024]{1,0:T(8,128)(2,1)S(1)}, u32[]{:S(2)}, u32[]{:S(2)}) collective-permute-start(bf16[128,1024]{1,0:T(8,128)(2,1)S(1)} %add_convert_fusion), channel_id=1, source_target_pairs={{0,16},{8,24},{16,0},{24,8},{1,17},{9,25},{17,1},{25,9},{2,18},{10... | collective-permute-start | bytes 786440 | tf_op jit(solution)/shard_map/ppermute | solution.py:256
  40.5 1.2 %collective-permute-start.8 = (f32[8,128]{1,0:T(8,128)S(1)}, f32[8,128]{1,0:T(8,128)S(1)}, u32[]{:S(2)}, u32[]{:S(2)}) collective-permute-start(f32[8,128]{1,0:T(8,128)S(1)} %get-tuple-element.44), channel_id=1, source_target_pairs={{0,1},{1,0},{2,3},{3,2},{4,5},{5,4},{6,7},{7,6},{8,9},{9,8},{10,11... | collective-permute-start | bytes 12296 | tf_op jit(solution)/shard_map/ppermute | solution.py:188
  41.7 3.6 %collective-permute-start.9 = (f32[8,128]{1,0:T(8,128)S(1)}, f32[8,128]{1,0:T(8,128)S(1)}, u32[]{:S(2)}, u32[]{:S(2)}) collective-permute-start(f32[8,128]{1,0:T(8,128)S(1)} %add.19), channel_id=1, source_target_pairs={{0,2},{1,3},{2,0},{3,1},{4,6},{5,7},{6,4},{7,5},{8,10},{9,11},{10,... | collective-permute-start | bytes 12296 | tf_op jit(solution)/shard_map/ppermute | solution.py:188
  45.3 4.5 %collective-permute-start.10 = (f32[8,128]{1,0:T(8,128)S(1)}, f32[8,128]{1,0:T(8,128)S(1)}, u32[]{:S(2)}, u32[]{:S(2)}) collective-permute-start(f32[8,128]{1,0:T(8,128)S(1)} %add.20), channel_id=1, source_target_pairs={{0,4},{1,5},{2,6},{3,7},{4,0},{5,1},{6,2},{7,3},{8,12},{9,13},{10,... | collective-permute-start | bytes 12296 | tf_op jit(solution)/shard_map/ppermute | solution.py:188
  49.8 3.6 %collective-permute-start.11 = (f32[8,128]{1,0:T(8,128)S(1)}, f32[8,128]{1,0:T(8,128)S(1)}, u32[]{:S(2)}, u32[]{:S(2)}) collective-permute-start(f32[8,128]{1,0:T(8,128)S(1)} %add.21), channel_id=1, source_target_pairs={{0,8},{8,0},{16,24},{24,16},{1,9},{9,1},{17,25},{25,17},{2,10},{10... | collective-permute-start | bytes 12296 | tf_op jit(solution)/shard_map/ppermute | solution.py:188
  53.4 3.6 %collective-permute-start.12 = (f32[8,128]{1,0:T(8,128)S(1)}, f32[8,128]{1,0:T(8,128)S(1)}, u32[]{:S(2)}, u32[]{:S(2)}) collective-permute-start(f32[8,128]{1,0:T(8,128)S(1)} %add.22), channel_id=1, source_target_pairs={{0,16},{8,24},{16,0},{24,8},{1,17},{9,25},{17,1},{25,9},{2,18},{10... | collective-permute-start | bytes 12296 | tf_op jit(solution)/shard_map/ppermute | solution.py:188
where the time goes:
time: 60.8 us; the launch traced here: 60.6 us
  waiting for transfers between devices  28.3 us (47%)
  starting transfers between devices  17.1 us (28%)
  Pallas kernels  13 us (21%)
  other arithmetic  1.08 us (2%)
  between operations  0.67 us (1%)
    pallas_call x5, Pallas kernels, call(): pl.pallas_call(kernel, in_specs=[pl.BlockSpec(memory_space=pltpu.SMEM)] *...  13 us
    ppermute x5, waiting for transfers between devices, moved(): return lax.ppermute(x, axis, pairs)  10.7 us
    ppermute x1, waiting for transfers between devices, per_device(): k2 = lax.ppermute(k, 'ctx', ahead)  6.52 us
    ppermute x5, starting transfers between devices, moved(): return lax.ppermute(x, axis, pairs)  5.81 us
    ppermute x1, waiting for transfers between devices, per_device(): ak = lax.ppermute(g1k, 'ctx', swap)  5.23 us
    ppermute x1, waiting for transfers between devices, per_device(): k1 = lax.ppermute(turned, 'ctx', swap)  3.07 us
    ppermute x1, starting transfers between devices, per_device(): k2 = lax.ppermute(k, 'ctx', ahead)  3.06 us
    ppermute x1, starting transfers between devices, per_device(): av = lax.ppermute(g1v, 'ctx', lead)  2.92 us
  transfers between devices with their start and end apart: 13, of which 9 were waited for; matrix products, arithmetic and copies ran while one was open for 1% of the time, Pallas kernels for 9%

commit v1 on v0

--- a/solution.py
+++ b/solution.py
@@ -60,7 +60,9 @@
 
 
 def prepare_kernel(first_ref, lengths_ref, q_ref, k_ref, v_ref, go_ref, qg_ref, kg_ref,
-                   q2_ref, qn_ref, kn_ref, s_ref, dp_ref, go2_ref, got_ref, v0_ref, bias_ref):
+                   q2_ref, qn_ref, kn_ref, s_ref, dp_ref, go2_ref, got_ref, v0_ref, bias_ref, k0_ref, kh_ref, ki_ref, qgo_ref, kgo_ref):
+    qgo_ref[...] = qg_ref[...]
+    kgo_ref[...] = kg_ref[...]
     rows = q_ref.shape[0]
 
     bias = mask_bias(lengths_ref, first_ref[0], WINDOW_SIZE + rows, rows)
@@ -74,8 +76,14 @@
         go2_ref[u] = go
         v0_ref[:, columns(u)] = v_ref[:, columns(u)]
         qn = (q * inverse_rms(q) * qg_ref[...]).astype(BF16)
-        k = k_ref[:, columns(u)].astype(F32)
-        kn = (k * inverse_rms(k) * kg_ref[...]).astype(BF16)
+        raw_k = k_ref[:, columns(u)]
+        k0_ref[:, columns(u)] = raw_k
+        k = raw_k.astype(F32)
+        k_inv = inverse_rms(k)
+        k_hat = k * k_inv
+        kh_ref[:, columns(u)] = k_hat
+        ki_ref[:, columns(u)] = jnp.broadcast_to(k_inv, k.shape)
+        kn = (k_hat * kg_ref[...]).astype(BF16)
         qn_ref[u] = qn
         kn_ref[:, columns(u)] = kn
         s_ref[u] = dot(kn, qn, 1, 1) * (score_scale * LOG2E) + bias
@@ -135,24 +143,22 @@
         dq = (q_inv * (t - q_hat * jnp.mean(t * q_hat, axis=-1, keepdims=True))).astype(BF16)
         for i in range(GROUP):
             dq_ref[:, columns(u * GROUP + i)] = dq[i * rows:(i + 1) * rows]
-    gains_ref[...] = jnp.zeros_like(gains_ref)
-    gains_ref[0:1, :] = q_part
-    gains_ref[1:2, :] = k_part / kg_ref[...]
+    parts = jnp.concatenate([q_part, k_part / kg_ref[...]], axis=0)
+    gains_ref[...] = jnp.broadcast_to(parts[None], gains_ref.shape)
 
 
 def value_kernel(dv_ref, a_ref, b_ref, out_ref):
     out_ref[...] = (dv_ref[...] + a_ref[...].astype(F32) + b_ref[...].astype(F32)).astype(BF16)
 
 
-def key_kernel(odd_ref, k_ref, dk_ref, a_ref, b_ref, kg_ref, out_ref):
+def key_kernel(odd_ref, kh_ref, ki_ref, dk_ref, a_ref, b_ref, kg_ref, out_ref):
     keep = (odd_ref[0] == 0).astype(F32)
-    for h in range(k_ref.shape[1] // HEAD_SIZE):
-        total = dk_ref[:, columns(h)] + a_ref[:, columns(h)].astype(F32) * keep + b_ref[:, columns(h)].astype(F32)
-        k = k_ref[:, columns(h)].astype(F32)
-        inv = inverse_rms(k)
-        k_hat = k * inv
+    for u in range(KEY_VALUE_HEADS):
+        total = dk_ref[:, columns(u)] + a_ref[:, columns(u)].astype(F32) * keep + b_ref[:, columns(u)].astype(F32)
+        k_hat = kh_ref[:, columns(u)]
         t = total * kg_ref[...]
-        out_ref[:, columns(h)] = (inv * (t - k_hat * jnp.mean(t * k_hat, axis=-1, keepdims=True))).astype(BF16)
+        dk = ki_ref[:, columns(u)] * (t - k_hat * jnp.mean(t * k_hat, axis=-1, keepdims=True))
+        out_ref[:, columns(u)] = dk.astype(BF16)
 
 
 def call(kernel, outs, args, scalars=()):
@@ -174,25 +180,6 @@
     return tuple(pltpu.with_memory_space_constraint(array, pltpu.HBM) for array in arrays)
 
 
-def sum_over(x, axis):
-    count, stride = lax.axis_size(axis), 1
-    while stride < count:
-        rest = count // stride
-        radix = next(f for f in range(2, rest + 1) if rest % f == 0)
-
-        def moved(turn):
-            pairs = []
-            for source in range(count):
-                digit = source // stride % radix
-                pairs.append((source, source + ((digit + turn) % radix - digit) * stride))
-            return lax.ppermute(x, axis, pairs)
-
-        parts = [moved(turn) for turn in range(1, radix)]
-        x = x + sum(parts)
-        stride = stride * radix
-    return x
-
-
 def per_device(queries, keys, values, grad_out, query_gain, key_gain, doc_lengths):
     rows = queries.shape[1]
     count = lax.axis_size("ctx")
@@ -211,21 +198,23 @@
 
     pair, keys, heads = GROUP * rows, WINDOW_SIZE + rows, KEY_VALUE_HEADS
     flat = (rows, heads * HEAD_SIZE)
+    devices = count * lax.axis_size("dp")
     tie = lax.optimization_barrier
 
     held, away = pltpu.VMEM, jax.ShapeDtypeStruct
     k2 = lax.ppermute(k, "ctx", ahead)
-    q2, qn, kn0, s0, dp0, go2, go_t, v0, bias = call(
+    q2, qn, kn0, s0, dp0, go2, go_t, v0, bias, k0, k_hat, k_inv, qg, kg = call(
         prepare_kernel,
         [
             held((heads, pair, HEAD_SIZE), BF16), held((heads, pair, HEAD_SIZE), BF16), held(flat, BF16),
             held((heads, rows, pair), F32), held((heads, rows, pair), F32),
             held((heads, pair, HEAD_SIZE), BF16), held((heads, HEAD_SIZE, pair), BF16),
-            held(flat, BF16), held((WINDOW_SIZE, rows), F32),
+            held(flat, BF16), held((WINDOW_SIZE, rows), F32), held(flat, BF16), held(flat, F32), held(flat, F32),
+            held((1, HEAD_SIZE), F32), held((1, HEAD_SIZE), F32),
         ],
         far(q, k, v, go, q_gain, k_gain), (first[None],) + far(doc_lengths),
     )
-    turned = jnp.where(odd == 1, k2, k)
+    turned = jnp.where(odd == 1, k2, k0)
     k1 = lax.ppermute(turned, "ctx", swap)
     late_v, _ = tie((v, turned))
     v2 = lax.ppermute(late_v, "ctx", ahead)
@@ -237,7 +226,7 @@
             held((keys, heads * HEAD_SIZE), BF16), held((heads, keys, pair), F32),
             held(flat, BF16), held(flat, BF16),
         ],
-        near(qn, kn0, s0, bias, k1, k2, go2) + far(k_gain),
+        near(qn, kn0, s0, bias, k1, k2, go2, kg),
     )
     av = lax.ppermute(g1v, "ctx", lead)
     bv = lax.ppermute(g2v, "ctx", behind)
@@ -246,20 +235,21 @@
         score_kernel,
         [
             held(flat, BF16), held(flat, BF16), away(q.shape, BF16),
-            held(flat, F32), held(flat, F32), held((8, HEAD_SIZE), F32),
+            held(flat, F32), held(flat, F32), held((devices, 2, HEAD_SIZE), F32),
         ],
-        near(p, v0, v1, v2, go2, go_t, dp0, q2, qn, kn) + far(q_gain, k_gain),
+        near(p, v0, v1, v2, go2, go_t, dp0, q2, qn, kn, qg, kg),
     )
     ak = lax.ppermute(g1k, "ctx", swap)
     keep = (odd == 1).astype(F32)
     joined = (g2k.astype(F32) + ak.astype(F32) * keep).astype(BF16)
     bk = lax.ppermute(joined, "ctx", behind)
-    gains = sum_over(sum_over(gains, "dp"), "ctx")
+    spread = lax.all_to_all(gains, ("ctx", "dp"), 0, 0)
+    gains = jnp.sum(spread, axis=0)
 
     dv = call(value_kernel, [away(flat, BF16)], near(dv_own, av, bv))[0]
     dk = call(
         key_kernel, [away(flat, BF16)],
-        far(k) + near(dk_own, ak, bk) + far(k_gain), (odd.astype(jnp.int32)[None],),
+        near(k_hat, k_inv, dk_own, ak, bk, kg), (odd.astype(jnp.int32)[None],),
     )[0]
     return (dq[None], dk[None], dv[None], gains[0], gains[1])
 

time: 60.8 us -> 55.6 us (0.914)
  the two profiles are of different devices: /device:TPU:0 before, /device:TPU:6 now
where the time goes in v1:
time: 55.6 us; the launch traced here: 55.5 us
  waiting for transfers between devices  27.4 us (49%)
  starting transfers between devices  14.8 us (27%)
  Pallas kernels  11.2 us (20%)
  other arithmetic  0.86 us (2%)
  between operations  0.67 us (1%)
    pallas_call x5, Pallas kernels, call(): pl.pallas_call(kernel, in_specs=[pl.BlockSpec(memory_space=pltpu.SMEM)] *...  11.2 us
    all_to_all x1, starting transfers between devices, per_device(): spread = lax.all_to_all(gains, ('ctx', 'dp'), 0, 0)  6.07 us
    ppermute x1, waiting for transfers between devices, per_device(): k1 = lax.ppermute(turned, 'ctx', swap)  5.69 us
    ppermute x1, waiting for transfers between devices, per_device(): bv = lax.ppermute(g2v, 'ctx', behind)  5.61 us
    ppermute x1, waiting for transfers between devices, per_device(): k2 = lax.ppermute(k, 'ctx', ahead)  5.34 us
    ppermute x1, waiting for transfers between devices, per_device(): bk = lax.ppermute(joined, 'ctx', behind)  4.09 us
    ppermute x1, waiting for transfers between devices, per_device(): av = lax.ppermute(g1v, 'ctx', lead)  3.83 us
    ppermute x1, starting transfers between devices, per_device(): v1 = lax.ppermute(late_v, 'ctx', follow)  2.67 us
  transfers between devices with their start and end apart: 9, of which 7 were waited for; matrix products, arithmetic and copies ran while one was open for 2% of the time, Pallas kernels for 10%

profile of v1, /device:TPU:6, one launch (start us, length us, event | category | flops | bytes accessed | tf_op | source)
XLA Modules:
  0.0 55.5 jit_solution(12658988836945418840)
XLA Ops:
  0.6 0.6 %collective-permute-start = (bf16[128,1024]{1,0:T(8,128)(2,1)}, bf16[128,1024]{1,0:T(8,128)(2,1)S(1)}, u32[]{:S(2)}, u32[]{:S(2)}) collective-permute-start(bf16[128,1024]{1,0:T(8,128)(2,1)} %bitcast.19), channel_id=1, source_target_pairs={{0,16},{8,24},{16,0},{24,8},{1,17},{9,25},{17,1},{25,9},{2,18},{10... | collective-permute-start | bytes 786440 | tf_op jit(solution)/shard_map/ppermute | solution.py:205
  1.2 2.4 %shard_map.110 = (bf16[8,256,128]{2,1,0:T(8,128)(2,1)S(1)}, bf16[8,256,128]{2,1,0:T(8,128)(2,1)S(1)}, bf16[128,1024]{1,0:T(8,128)(2,1)S(1)}, f32[8,128,256]{2,1,...) custom-call(s32[1]{0:T(128)} %bitcast.first_ref, ...), custom_call_target="tpu_custom_call" | custom-call | tf_op jit(solution)/shard_map/pallas_call | solution.py:166
  3.6 5.3 %collective-permute-done.k2_ref = bf16[128,1024]{1,0:T(8,128)(2,1)S(1)} collective-permute-done((bf16[128,1024]{1,0:T(8,128)(2,1)}, bf16[128,1024]{1,0:T(8,128)(2,1)S(1)}, u32[]{:S(2)}, u32[]{:S(2)}) %collective-permute-start) | collective-permute-done | bytes 262176 | tf_op jit(solution)/shard_map/ppermute | solution.py:205
  9.0 0.6 %collective-permute-start.1 = (bf16[128,1024]{1,0:T(8,128)(2,1)S(1)}, bf16[128,1024]{1,0:T(8,128)(2,1)S(1)}, u32[]{:S(2)}, u32[]{:S(2)}) collective-permute-start(bf16[128,1024]{1,0:T(8,128)(2,1)S(1)} %broadcast_select_fusion), channel_id=1, source_target_pairs={{0,8},{8,0},{16,24},{24,16},{1,9},{9,1},{17,25},{25,17},{2,10},{10... | collective-permute-start | bytes 786440 | tf_op jit(solution)/shard_map/ppermute | solution.py:218
  9.6 0.3 collective-permute-start.3
  9.9 2.7 %collective-permute-start.2 = (bf16[128,1024]{1,0:T(8,128)(2,1)}, bf16[128,1024]{1,0:T(8,128)(2,1)S(1)}, u32[]{:S(2)}, u32[]{:S(2)}) collective-permute-start(bf16[128,1024]{1,0:T(8,128)(2,1)} %bitcast.23), channel_id=1, source_target_pairs={{0,8},{8,16},{16,24},{24,0},{1,9},{9,17},{17,25},{25,1},{2,10},{10... | collective-permute-start | bytes 786440 | tf_op jit(solution)/shard_map/ppermute | solution.py:221
  12.5 5.7 %collective-permute-done.1.k1_ref = bf16[128,1024]{1,0:T(8,128)(2,1)S(1)} collective-permute-done((bf16[128,1024]{1,0:T(8,128)(2,1)S(1)}, bf16[128,1024]{1,0:T(8,128)(2,1)S(1)}, u32[]{:S(2)}, u32[]{:S(2)}) %collective-permute-start.1) | collective-permute-done | bytes 262176 | tf_op jit(solution)/shard_map/ppermute | solution.py:218
  18.2 2.6 %shard_map.111 = (bf16[384,1024]{1,0:T(8,128)(2,1)S(1)}, f32[8,384,256]{2,1,0:T(8,128)S(1)}, bf16[128,1024]{1,0:T(8,128)(2,1)}, bf16[128,1024]{1,0:T(8,128)(2,1)S(1)}) custom-call(bf16[8,256,128]{2,1,0:T(8,128)(2,1)S(1)} %get-tuple-element.30.qn_ref, bf16[128,1024]{1,0:T(8,128)(2,1)S(1)} %get-tuple-element.31.kn0_ref, ...), custom_call_target="tpu_custom_call" | custom-call | tf_op jit(solution)/shard_map/pallas_call | solution.py:166
  20.8 0.0 collective-permute-done.3.v2_ref
  20.8 1.1 %collective-permute-done.2.v1_ref = bf16[128,1024]{1,0:T(8,128)(2,1)S(1)} collective-permute-done((bf16[128,1024]{1,0:T(8,128)(2,1)}, bf16[128,1024]{1,0:T(8,128)(2,1)S(1)}, u32[]{:S(2)}, u32[]{:S(2)}) %collective-permute-start.2) | collective-permute-done | bytes 262176 | tf_op jit(solution)/shard_map/ppermute | solution.py:221
  21.9 4.5 %shard_map.112 = (bf16[128,1024]{1,0:T(8,128)(2,1)}, bf16[128,1024]{1,0:T(8,128)(2,1)S(1)}, bf16[128,2048]{1,0:T(8,128)(2,1)}, f32[128,1024]{1,0:T(8,128)S(1)}, ...) custom-call(f32[8,384,256]{2,1,0:T(8,128)S(1)} %get-tuple-element.37.p_ref, ...), custom_call_target="tpu_custom_call" | custom-call | tf_op jit(solution)/shard_map/pallas_call | solution.py:166
  26.3 2.0 %collective-permute-start.4 = (bf16[128,1024]{1,0:T(8,128)(2,1)}, bf16[128,1024]{1,0:T(8,128)(2,1)S(1)}, u32[]{:S(2)}, u32[]{:S(2)}) collective-permute-start(bf16[128,1024]{1,0:T(8,128)(2,1)} %get-tuple-element.49), channel_id=1, source_target_pairs={{0,8},{8,0},{16,24},{24,16},{1,9},{9,1},{17,25},{25,17},{2,10},{10... | collective-permute-start | bytes 786440 | tf_op jit(solution)/shard_map/ppermute | solution.py:242
  28.3 6.1 %all-to-all-start = ((f32[32,2,128]{2,1,0:T(2,128)}), f32[32,2,128]{2,1,0:T(2,128)S(1)}, u32[]{:S(2)}, u32[]{:S(2)}) async-start(f32[32,2,128]{2,1,0:T(2,128)} %get-tuple-element.54), calls=%async_computation | async-start | bytes 65536 | tf_op jit(solution)/shard_map/all_to_all | solution.py:246
  34.4 0.6 %collective-permute-start.6 = (bf16[128,1024]{1,0:T(8,128)(2,1)}, bf16[128,1024]{1,0:T(8,128)(2,1)S(1)}, u32[]{:S(2)}, u32[]{:S(2)}) collective-permute-start(bf16[128,1024]{1,0:T(8,128)(2,1)} %get-tuple-element.52), channel_id=1, source_target_pairs={{0,24},{8,0},{16,8},{24,16},{1,25},{9,1},{17,9},{25,17},{2,26},{10... | collective-permute-start | bytes 786440 | tf_op jit(solution)/shard_map/ppermute | solution.py:231
  35.0 0.3 collective-permute-start.7
  35.2 0.8 %add_convert_fusion = bf16[128,1024]{1,0:T(8,128)(2,1)} fusion(bf16[128,1024]{1,0:T(8,128)(2,1)S(1)} %collective-permute-done.4.a_ref, bf16[128,1024]{1,0:T(8,128)(2,1)S(1)} %get-tuple-element.50, f32[]{:T(128)S(6)} %convert_element_type.14), kind=kLoop, calls=%fused_computation | loop fusion | flops 655360 | bytes 786436 | tf_op jit(solution)/shard_map/convert_element_type | solution.py:244
  36.0 1.8 %collective-permute-start.5 = (bf16[128,1024]{1,0:T(8,128)(2,1)}, bf16[128,1024]{1,0:T(8,128)(2,1)S(1)}, u32[]{:S(2)}, u32[]{:S(2)}) collective-permute-start(bf16[128,1024]{1,0:T(8,128)(2,1)} %add_convert_fusion), channel_id=1, source_target_pairs={{0,16},{8,24},{16,0},{24,8},{1,17},{9,25},{17,1},{25,9},{2,18},{10... | collective-permute-start | bytes 786440 | tf_op jit(solution)/shard_map/ppermute | solution.py:245
  37.8 1.8 %all-to-all-done = f32[32,2,128]{2,1,0:T(2,128)S(1)} async-done(((f32[32,2,128]{2,1,0:T(2,128)}), f32[32,2,128]{2,1,0:T(2,128)S(1)}, u32[]{:S(2)}, u32[]{:S(2)}) %all-to-all-start) | async-done | bytes 32800 | tf_op jit(solution)/shard_map/all_to_all | solution.py:246
  39.6 0.5 slice_bitcast_fusion
  40.2 3.8 %collective-permute-done.6.a_ref = bf16[128,1024]{1,0:T(8,128)(2,1)S(1)} collective-permute-done((bf16[128,1024]{1,0:T(8,128)(2,1)}, bf16[128,1024]{1,0:T(8,128)(2,1)S(1)}, u32[]{:S(2)}, u32[]{:S(2)}) %collective-permute-start.6) | collective-permute-done | bytes 262176 | tf_op jit(solution)/shard_map/ppermute | solution.py:231
  44.0 5.6 %collective-permute-done.7.b_ref = bf16[128,1024]{1,0:T(8,128)(2,1)S(1)} collective-permute-done((bf16[128,1024]{1,0:T(8,128)(2,1)S(1)}, bf16[128,1024]{1,0:T(8,128)(2,1)S(1)}, u32[]{:S(2)}, u32[]{:S(2)}) %collective-permute-start.7) | collective-permute-done | bytes 262176 | tf_op jit(solution)/shard_map/ppermute | solution.py:232
  49.6 0.8 %shard_map.114 = bf16[128,1024]{1,0:T(8,128)(2,1)} custom-call(f32[128,1024]{1,0:T(8,128)S(1)} %get-tuple-element.51.dv_ref, bf16[128,1024]{1,0:T(8,128)(2,1)S(1)} %collective-permute-done.6.a_ref, bf16[128,1024]{1,0:T(8,128)(2,1)S(1)} %collective-permute-done.7.b_ref), custom_call_target="tpu_custom_call" | custom-call | tf_op jit(solution)/shard_map/pallas_call | solution.py:166
  50.4 4.1 %collective-permute-done.5.b_ref = bf16[128,1024]{1,0:T(8,128)(2,1)S(1)} collective-permute-done((bf16[128,1024]{1,0:T(8,128)(2,1)}, bf16[128,1024]{1,0:T(8,128)(2,1)S(1)}, u32[]{:S(2)}, u32[]{:S(2)}) %collective-permute-start.5) | collective-permute-done | bytes 262176 | tf_op jit(solution)/shard_map/ppermute | solution.py:245
  54.5 1.0 %shard_map.113 = bf16[128,1024]{1,0:T(8,128)(2,1)} custom-call(s32[1]{0:T(128)} %bitcast.8.odd_ref, f32[128,1024]{1,0:T(8,128)S(1)} %get-tuple-element.46.kh_ref, f32[128,1024]{1,0:T(8,128)S(1)} %get-tuple-element.47.ki_ref, f32[128,1024]{1,0:T(8,128)S(1)} %get-tuple-element.48.dk_ref, bf16[128,1024]{1,0:T(8,128)(2,1)S(1)} %collective-permute-done.4.a_ref, ...), custom_call_target="tpu_custom_call" | custom-call | tf_op jit(solution)/shard_map/pallas_call | solution.py:166
  (3 shorter events, 0.1 us)
Async XLA Ops:
  0.6 8.3 %collective-permute-start = (bf16[128,1024]{1,0:T(8,128)(2,1)}, bf16[128,1024]{1,0:T(8,128)(2,1)S(1)}, u32[]{:S(2)}, u32[]{:S(2)}) collective-permute-start(bf16[128,1024]{1,0:T(8,128)(2,1)} %bitcast.19), channel_id=1, source_target_pairs={{0,16},{8,24},{16,0},{24,8},{1,17},{9,25},{17,1},{25,9},{2,18},{10... | collective-permute-start | bytes 786440 | tf_op jit(solution)/shard_map/ppermute | solution.py:205
  9.0 9.2 %collective-permute-start.1 = (bf16[128,1024]{1,0:T(8,128)(2,1)S(1)}, bf16[128,1024]{1,0:T(8,128)(2,1)S(1)}, u32[]{:S(2)}, u32[]{:S(2)}) collective-permute-start(bf16[128,1024]{1,0:T(8,128)(2,1)S(1)} %broadcast_select_fusion), channel_id=1, source_target_pairs={{0,8},{8,0},{16,24},{24,16},{1,9},{9,1},{17,25},{25,17},{2,10},{10... | collective-permute-start | bytes 786440 | tf_op jit(solution)/shard_map/ppermute | solution.py:218
  9.6 11.2 %collective-permute-start.3 = (bf16[128,1024]{1,0:T(8,128)(2,1)}, bf16[128,1024]{1,0:T(8,128)(2,1)S(1)}, u32[]{:S(2)}, u32[]{:S(2)}) collective-permute-start(bf16[128,1024]{1,0:T(8,128)(2,1)} %bitcast.22), channel_id=1, source_target_pairs={{0,16},{8,24},{16,0},{24,8},{1,17},{9,25},{17,1},{25,9},{2,18},{10... | collective-permute-start | bytes 786440 | tf_op jit(solution)/shard_map/ppermute | solution.py:220
  9.9 12.0 %collective-permute-start.2 = (bf16[128,1024]{1,0:T(8,128)(2,1)}, bf16[128,1024]{1,0:T(8,128)(2,1)S(1)}, u32[]{:S(2)}, u32[]{:S(2)}) collective-permute-start(bf16[128,1024]{1,0:T(8,128)(2,1)} %bitcast.23), channel_id=1, source_target_pairs={{0,8},{8,16},{16,24},{24,0},{1,9},{9,17},{17,25},{25,1},{2,10},{10... | collective-permute-start | bytes 786440 | tf_op jit(solution)/shard_map/ppermute | solution.py:221
  26.3 8.9 %collective-permute-start.4 = (bf16[128,1024]{1,0:T(8,128)(2,1)}, bf16[128,1024]{1,0:T(8,128)(2,1)S(1)}, u32[]{:S(2)}, u32[]{:S(2)}) collective-permute-start(bf16[128,1024]{1,0:T(8,128)(2,1)} %get-tuple-element.49), channel_id=1, source_target_pairs={{0,8},{8,0},{16,24},{24,16},{1,9},{9,1},{17,25},{25,17},{2,10},{10... | collective-permute-start | bytes 786440 | tf_op jit(solution)/shard_map/ppermute | solution.py:242
  28.3 11.3 %all-to-all-start = ((f32[32,2,128]{2,1,0:T(2,128)}), f32[32,2,128]{2,1,0:T(2,128)S(1)}, u32[]{:S(2)}, u32[]{:S(2)}) async-start(f32[32,2,128]{2,1,0:T(2,128)} %get-tuple-element.54), calls=%async_computation | async-start | bytes 65536 | tf_op jit(solution)/shard_map/all_to_all | solution.py:246
  34.4 9.6 %collective-permute-start.6 = (bf16[128,1024]{1,0:T(8,128)(2,1)}, bf16[128,1024]{1,0:T(8,128)(2,1)S(1)}, u32[]{:S(2)}, u32[]{:S(2)}) collective-permute-start(bf16[128,1024]{1,0:T(8,128)(2,1)} %get-tuple-element.52), channel_id=1, source_target_pairs={{0,24},{8,0},{16,8},{24,16},{1,25},{9,1},{17,9},{25,17},{2,26},{10... | collective-permute-start | bytes 786440 | tf_op jit(solution)/shard_map/ppermute | solution.py:231
  35.0 14.6 %collective-permute-start.7 = (bf16[128,1024]{1,0:T(8,128)(2,1)S(1)}, bf16[128,1024]{1,0:T(8,128)(2,1)S(1)}, u32[]{:S(2)}, u32[]{:S(2)}) collective-permute-start(bf16[128,1024]{1,0:T(8,128)(2,1)S(1)} %get-tuple-element.53), channel_id=1, source_target_pairs={{0,16},{8,24},{16,0},{24,8},{1,17},{9,25},{17,1},{25,9},{2,18},{10... | collective-permute-start | bytes 786440 | tf_op jit(solution)/shard_map/ppermute | solution.py:232
  36.0 18.5 %collective-permute-start.5 = (bf16[128,1024]{1,0:T(8,128)(2,1)}, bf16[128,1024]{1,0:T(8,128)(2,1)S(1)}, u32[]{:S(2)}, u32[]{:S(2)}) collective-permute-start(bf16[128,1024]{1,0:T(8,128)(2,1)} %add_convert_fusion), channel_id=1, source_target_pairs={{0,16},{8,24},{16,0},{24,8},{1,17},{9,25},{17,1},{25,9},{2,18},{10... | collective-permute-start | bytes 786440 | tf_op jit(solution)/shard_map/ppermute | solution.py:245

commit v2 on v1

v2 whole, which is shorter than its diff:
```python
import jax
import jax.numpy as jnp
from jax import lax
from jax.experimental import pallas as pl
from jax.experimental.pallas import tpu as pltpu
from jax.sharding import PartitionSpec as P


QUERY_HEADS = 16
KEY_VALUE_HEADS = 8
HEAD_SIZE = 128
WINDOW_SIZE = 256
GROUP = QUERY_HEADS // KEY_VALUE_HEADS

norm_epsilon = 1e-06
score_scale = 168.0 ** (-0.5)
MASKED = -1e30
LOG2E = 1.4426950408889634
VMEM_LIMIT = 16 << 20


F32 = jnp.float32
BF16 = jnp.bfloat16


def dot(a, b, ca, cb):
    return lax.dot_general(a, b, (((ca,), (cb,)), ((), ())), preferred_element_type=F32)


def inverse_rms(x):
    return lax.rsqrt(jnp.mean(x * x, axis=-1, keepdims=True) + norm_epsilon)


def document_of(lengths_ref, positions):
    index = jnp.zeros(positions.shape, jnp.int32)
    end = jnp.int32(0)
    for doc in range(lengths_ref.shape[1]):
        end = end + lengths_ref[0, doc]
        index = index + (positions >= end).astype(jnp.int32)
    return index


def mask_bias(lengths_ref, first, keys, rows):
    key_pos = first - WINDOW_SIZE + lax.broadcasted_iota(jnp.int32, (keys, 1), 0)
    query_pos = first + lax.broadcasted_iota(jnp.int32, (1, rows), 1)
    key_doc = jnp.where(key_pos >= 0, document_of(lengths_ref, key_pos), -1)
    query_doc = document_of(lengths_ref, query_pos)
    gap = query_pos - key_pos
    allowed = (key_doc == query_doc) & (gap >= 0) & (gap < WINDOW_SIZE)
    return jnp.where(allowed, 0.0, MASKED).astype(F32)


def stacked(ref, u):
    parts = [ref[:, (u * GROUP + i) * HEAD_SIZE:(u * GROUP + i + 1) * HEAD_SIZE] for i in range(GROUP)]
    return jnp.concatenate(parts, axis=0)


def columns(u):
    return slice(u * HEAD_SIZE, (u + 1) * HEAD_SIZE)


def prepare_kernel(first_ref, lengths_ref, q_ref, k_ref, v_ref, go_ref, qg_ref, kg_ref,
                   qh_ref, qn_ref, kn_ref, s_ref, dp_ref, go2_ref, got_ref, v0_ref, bias_ref, k0_ref, qgo_ref, kgo_ref):
    qgo_ref[...] = qg_ref[...]
    kgo_ref[...] = kg_ref[...]
    rows = q_ref.shape[0]

    bias = mask_bias(lengths_ref, first_ref[0], WINDOW_SIZE + rows, rows)
    bias_ref[...] = bias[:WINDOW_SIZE]
    bias = jnp.concatenate([bias[WINDOW_SIZE:]] * GROUP, axis=1)
    for u in range(KEY_VALUE_HEADS):
        raw = stacked(q_ref, u)
        q = raw.astype(F32)
        q_inv = inverse_rms(q)
        q_hat = q * q_inv
        qh_ref[u] = q_hat
        go = stacked(go_ref, u)
        go2_ref[u] = go
        v0_ref[:, columns(u)] = v_ref[:, columns(u)]
        qn = (q_hat * qg_ref[...]).astype(BF16)
        raw_k = k_ref[:, columns(u)]
        k0_ref[:, columns(u)] = raw_k
        k = raw_k.astype(F32)
        kn = (k * inverse_rms(k) * kg_ref[...]).astype(BF16)
        qn_ref[u] = qn
        kn_ref[:, columns(u)] = kn
        s_ref[u] = dot(kn, qn, 1, 1) * (score_scale * LOG2E) + bias
        dp_ref[u] = dot(v_ref[:, columns(u)], go, 1, 1)
        got_ref[u] = jnp.transpose(go)


def early_kernel(qn_ref, s_ref, bias_ref, k2_ref, kg_ref, kn_ref, e_ref, top_ref, sum_ref):
    rows = k2_ref.shape[0]
    bias = jnp.concatenate([bias_ref[:rows]] * GROUP, axis=1)
    for u in range(KEY_VALUE_HEADS):
        k = k2_ref[:, columns(u)].astype(F32)
        kn = (k * inverse_rms(k) * kg_ref[...]).astype(BF16)
        kn_ref[:, columns(u)] = kn
        s2 = dot(kn, qn_ref[u], 1, 1) * (score_scale * LOG2E) + bias
        s0 = s_ref[u]
        top = jnp.maximum(jnp.max(s2, axis=0, keepdims=True), jnp.max(s0, axis=0, keepdims=True))
        e2, e0 = jnp.exp2(s2 - top), jnp.exp2(s0 - top)
        e_ref[u, :rows] = e2
        e_ref[u, rows:] = e0
        top_ref[u] = top
        sum_ref[u] = jnp.sum(e2, axis=0, keepdims=True) + jnp.sum(e0, axis=0, keepdims=True)


def weigh_kernel(qn_ref, e_ref, top_ref, sum_ref, bias_ref, k1_ref, go_ref, kg_ref, kn_ref, p_ref, low_ref, g1v_ref, g2v_ref):
    rows = k1_ref.shape[0]
    bias = jnp.concatenate([bias_ref[rows:]] * GROUP, axis=1)
    for u in range(KEY_VALUE_HEADS):
        k = k1_ref[:, columns(u)].astype(F32)
        kn = (k * inverse_rms(k) * kg_ref[...]).astype(BF16)
        kn_ref[:, columns(u)] = kn
        s1 = dot(kn, qn_ref[u], 1, 1) * (score_scale * LOG2E) + bias
        top = jnp.maximum(top_ref[u], jnp.max(s1, axis=0, keepdims=True))
        e1 = jnp.exp2(s1 - top)
        fade = jnp.exp2(top_ref[u] - top)
        inv = 1.0 / (sum_ref[u] * fade + jnp.sum(e1, axis=0, keepdims=True))
        fade = fade * inv
        p2 = e_ref[u, :rows] * fade
        p1 = e1 * inv
        p_ref[u, :rows] = p2
        p_ref[u, rows:WINDOW_SIZE] = p1
        p0 = e_ref[u, rows:] * fade
        p_ref[u, WINDOW_SIZE:] = p0
        low_ref[u] = p0.astype(BF16)
        g1v_ref[:, columns(u)] = dot(p1.astype(BF16), go_ref[u], 1, 0).astype(BF16)
        g2v_ref[:, columns(u)] = dot(p2.astype(BF16), go_ref[u], 1, 0).astype(BF16)


def score_kernel(p_ref, low_ref, v0_ref, v1_ref, v2_ref, go_ref, got_ref, dp_ref, qh_ref, qn_ref, kn2_ref, kn1_ref, kn0_ref,
                 kg_ref, g1k_ref, g2k_ref, ds_ref, dqn_ref, gains_ref):
    rows = v0_ref.shape[0]
    q_part = jnp.zeros((1, HEAD_SIZE), F32)
    k_part = jnp.zeros((1, HEAD_SIZE), F32)
    for u in range(KEY_VALUE_HEADS):
        v = jnp.concatenate([v2_ref[:, columns(u)], v1_ref[:, columns(u)]], axis=0)
        qn = qn_ref[u]
        p, p0 = p_ref[u, :WINDOW_SIZE], p_ref[u, WINDOW_SIZE:]
        attended = dot(v, p.astype(BF16), 0, 0) + dot(v0_ref[:, columns(u)], low_ref[u], 0, 0)
        attended = attended.astype(BF16).astype(F32)
        delta = jnp.sum(got_ref[u].astype(F32) * attended, axis=0, keepdims=True)
        ds = (p * (dot(v, go_ref[u], 1, 1) - delta)).astype(BF16)
        ds0 = (p0 * (dp_ref[u] - delta)).astype(BF16)
        ds_ref[u] = ds0
        g = (dot(ds, qn, 1, 0) * score_scale).astype(BF16)
        g2k_ref[:, columns(u)] = g[:rows]
        g1k_ref[:, columns(u)] = g[rows:]
        kn = jnp.concatenate([ref[:, columns(u)] for ref in (kn2_ref, kn1_ref, kn0_ref)], axis=0)
        dqn = dot(jnp.concatenate([ds, ds0], axis=0), kn, 0, 0) * score_scale
        dqn_ref[u] = dqn
        q_part = q_part + jnp.sum(dqn * qh_ref[u], axis=0, keepdims=True)
        k_part = k_part + jnp.sum(dqn * qn.astype(F32), axis=0, keepdims=True)
    parts = jnp.concatenate([q_part, k_part / kg_ref[...]], axis=0)
    gains_ref[...] = jnp.broadcast_to(parts[None], gains_ref.shape)


def rest_kernel(q_ref, go_ref, low_ref, ds_ref, dqn_ref, qg_ref, a_ref, b_ref,
                dq_ref, dk_ref, dv_ref):
    rows = a_ref.shape[0]
    for u in range(KEY_VALUE_HEADS):
        own = dot(low_ref[u], stacked(go_ref, u), 1, 0)
        total = own + a_ref[:, columns(u)].astype(F32) + b_ref[:, columns(u)].astype(F32)
        dv_ref[:, columns(u)] = total.astype(BF16)
        q = stacked(q_ref, u).astype(F32)
        q_inv = inverse_rms(q)
        q_hat = q * q_inv
        dk_ref[:, columns(u)] = dot(ds_ref[u], (q_hat * qg_ref[...]).astype(BF16), 1, 0) * score_scale
        t = dqn_ref[u] * qg_ref[...]
        dq = (q_inv * (t - q_hat * jnp.mean(t * q_hat, axis=-1, keepdims=True))).astype(BF16)
        for i in range(GROUP):
            dq_ref[:, columns(u * GROUP + i)] = dq[i * rows:(i + 1) * rows]


def turn_kernel(odd_ref, own_ref, got_ref, out_ref):
    out_ref[...] = jnp.where(odd_ref[0] == 1, got_ref[...], own_ref[...])


def join_kernel(odd_ref, own_ref, got_ref, out_ref):
    keep = (odd_ref[0] == 1).astype(F32)
    out_ref[...] = (own_ref[...].astype(F32) + got_ref[...].astype(F32) * keep).astype(BF16)


def total_kernel(k_ref, parts_ref, q_out_ref, k_out_ref, kh_ref, ki_ref):
    total = jnp.sum(parts_ref[...], axis=0)
    q_out_ref[...] = total[0:1]
    k_out_ref[...] = total[1:2]
    for u in range(KEY_VALUE_HEADS):
        k = k_ref[:, columns(u)].astype(F32)
        k_inv = inverse_rms(k)
        kh_ref[:, columns(u)] = k * k_inv
        ki_ref[:, columns(u)] = jnp.broadcast_to(k_inv, k.shape)


def key_kernel(odd_ref, kh_ref, ki_ref, dk_ref, a_ref, b_ref, kg_ref, out_ref):
    keep = (odd_ref[0] == 0).astype(F32)
    for u in range(KEY_VALUE_HEADS):
        total = dk_ref[:, columns(u)] + a_ref[:, columns(u)].astype(F32) * keep + b_ref[:, columns(u)].astype(F32)
        k_hat = kh_ref[:, columns(u)]
        t = total * kg_ref[...]
        dk = ki_ref[:, columns(u)] * (t - k_hat * jnp.mean(t * k_hat, axis=-1, keepdims=True))
        out_ref[:, columns(u)] = dk.astype(BF16)


def call(kernel, outs, args, scalars=()):
    vmem = pl.BlockSpec(memory_space=pltpu.VMEM)
    return pl.pallas_call(
        kernel,
        in_specs=[pl.BlockSpec(memory_space=pltpu.SMEM)] * len(scalars) + [vmem] * len(args),
        out_specs=[vmem] * len(outs),
        out_shape=outs,
        compiler_params=pltpu.CompilerParams(vmem_limit_bytes=VMEM_LIMIT),
    )(*scalars, *args)


def near(*arrays):
    return tuple(pltpu.with_memory_space_constraint(array, pltpu.VMEM) for array in arrays)


def far(*arrays):
    return tuple(pltpu.with_memory_space_constraint(array, pltpu.HBM) for array in arrays)


def per_device(queries, keys, values, grad_out, query_gain, key_gain, doc_lengths):
    rows = queries.shape[1]
    count = lax.axis_size("ctx")
    assert rows * 2 == WINDOW_SIZE and count % 2 == 0
    here = lax.axis_index("ctx")
    odd = lax.rem(here, 2)
    first = (here * rows).astype(jnp.int32)
    q, k, v, go = queries[0], keys[0], values[0], grad_out[0]
    q_gain, k_gain = query_gain[None], key_gain[None]

    ahead = [(i, (i + 2) % count) for i in range(count)]
    behind = [(i, (i - 2) % count) for i in range(count)]
    follow = [(i, (i + 1) % count) for i in range(count)]
    lead = [(i, (i - 1) % count) for i in range(count)]
    swap = [(i, i ^ 1) for i in range(count)]

    pair, keys, heads = GROUP * rows, WINDOW_SIZE + rows, KEY_VALUE_HEADS
    flat = (rows, heads * HEAD_SIZE)
    devices = count * lax.axis_size("dp")
    parity = odd.astype(jnp.int32)[None]

    held, away = pltpu.VMEM, jax.ShapeDtypeStruct
    k2 = lax.ppermute(k, "ctx", ahead)
    q_hat, qn, kn0, s0, dp0, go2, go_t, v0, bias, k0, qg, kg = call(
        prepare_kernel,
        [
            held((heads, pair, HEAD_SIZE), F32),
            held((heads, pair, HEAD_SIZE), BF16), held(flat, BF16),
            held((heads, rows, pair), F32), held((heads, rows, pair), F32),
            held((heads, pair, HEAD_SIZE), BF16), held((heads, HEAD_SIZE, pair), BF16),
            held(flat, BF16), held((WINDOW_SIZE, rows), F32), held(flat, BF16),
            held((1, HEAD_SIZE), F32), held((1, HEAD_SIZE), F32),
        ],
        far(q, k, v, go, q_gain, k_gain), (first[None],) + far(doc_lengths),
    )
    turned = call(turn_kernel, [held(flat, BF16)], near(k0, k2), (parity,))[0]
    k1 = lax.ppermute(turned, "ctx", swap)
    v2 = lax.ppermute(v, "ctx", ahead)
    v1 = lax.ppermute(v, "ctx", follow)

    kn2, e, top, norm = call(
        early_kernel,
        [
            held(flat, BF16), held((heads, WINDOW_SIZE, pair), F32),
            held((heads, 1, pair), F32), held((heads, 1, pair), F32),
        ],
        near(qn, s0, bias, k2, kg),
    )
    kn1, p, p_low, g1v, g2v = call(
        weigh_kernel,
        [
            held(flat, BF16), held((heads, keys, pair), F32), held((heads, rows, pair), BF16),
            held(flat, BF16), held(flat, BF16),
        ],
        near(qn, e, top, norm, bias, k1, go2, kg),
    )
    av = lax.ppermute(g1v, "ctx", lead)
    bv = lax.ppermute(g2v, "ctx", behind)

    g1k, g2k, ds0, dqn, gains = call(
        score_kernel,
        [
            held(flat, BF16), held(flat, BF16), held((heads, rows, pair), BF16),
            held((heads, pair, HEAD_SIZE), F32), held((devices, 2, HEAD_SIZE), F32),
        ],
        near(p, p_low, v0, v1, v2, go2, go_t, dp0, q_hat, qn, kn2, kn1, kn0, kg),
    )
    ak = lax.ppermute(g1k, "ctx", swap)
    joined = call(join_kernel, [held(flat, BF16)], near(g2k, ak), (parity,))[0]
    bk = lax.ppermute(joined, "ctx", behind)
    spread = lax.all_to_all(gains, ("ctx", "dp"), 0, 0)
    line = away((1, HEAD_SIZE), F32)
    q_total, k_total, k_hat, k_inv = call(
        total_kernel, [line, line, held(flat, F32), held(flat, F32)], far(k) + near(spread)
    )

    dq, dk_own, dv = call(
        rest_kernel, [away(q.shape, BF16), held(flat, F32), away(flat, BF16)],
        far(q, go) + near(p_low, ds0, dqn, qg) + far(av, bv),
    )
    dk = call(
        key_kernel, [away(flat, BF16)],
        near(k_hat, k_inv, dk_own, ak, bk, kg), (parity,),
    )[0]
    return (dq[None], dk[None], dv[None], q_total[0], k_total[0])


def solution(mesh):
    in_specs = (
        P("dp", "ctx", None),
        P("dp", "ctx", None),
        P("dp", "ctx", None),
        P("dp", "ctx", None),
        P(),
        P(),
        P("dp", None),
    )
    out_specs = (P("dp", "ctx", None), P("dp", "ctx", None), P("dp", "ctx", None), P(), P())
    return jax.shard_map(
        per_device, mesh=mesh, in_specs=in_specs, out_specs=out_specs, check_vma=False
    )
```

time: 55.6 us -> 56.1 us (level)
  the two profiles are of different devices: /device:TPU:6 before, /device:TPU:0 now
where the time goes in v2:
time: 56.1 us; the launch traced here: 55.9 us
  waiting for transfers between devices  17.1 us (30%)
  Pallas kernels  14.3 us (25%)
  blocking collectives  11.6 us (21%)
  starting transfers between devices  11.3 us (20%)
  local copies, waits for them, and re-layouts  0.77 us (1%)
  between operations  0.69 us (1%)
    pallas_call x9, Pallas kernels, call(): pl.pallas_call(kernel, in_specs=[pl.BlockSpec(memory_space=pltpu.SMEM)] *...  14.3 us
    all_to_all x1, blocking collectives, per_device(): spread = lax.all_to_all(gains, ('ctx', 'dp'), 0, 0)  11.6 us
    ppermute x1, waiting for transfers between devices, per_device(): ak = lax.ppermute(g1k, 'ctx', swap)  4.92 us
    ppermute x1, waiting for transfers between devices, per_device(): k1 = lax.ppermute(turned, 'ctx', swap)  4.69 us
    ppermute x1, waiting for transfers between devices, per_device(): k2 = lax.ppermute(k, 'ctx', ahead)  4.13 us
    ppermute x1, starting transfers between devices, per_device(): k2 = lax.ppermute(k, 'ctx', ahead)  3.06 us
    ppermute x1, starting transfers between devices, per_device(): av = lax.ppermute(g1v, 'ctx', lead)  2.91 us
    ppermute x1, waiting for transfers between devices, per_device(): v1 = lax.ppermute(v, 'ctx', follow)  2.69 us
  transfers between devices with their start and end apart: 8, of which 5 were waited for; matrix products, arithmetic and copies ran while one was open for 0% of the time, Pallas kernels for 18%

profile of v2, /device:TPU:0, one launch (start us, length us, event | category | flops | bytes accessed | tf_op | source)
XLA Modules:
  0.0 55.9 jit_solution(6133960593790048806)
XLA Ops:
  0.6 3.1 %collective-permute-start = (bf16[128,1024]{1,0:T(8,128)(2,1)}, bf16[128,1024]{1,0:T(8,128)(2,1)S(1)}, u32[]{:S(2)}, u32[]{:S(2)}) collective-permute-start(bf16[128,1024]{1,0:T(8,128)(2,1)} %bitcast.17), channel_id=1, source_target_pairs={{0,16},{8,24},{16,0},{24,8},{1,17},{9,25},{17,1},{25,9},{2,18},{10... | collective-permute-start | bytes 786440 | tf_op jit(solution)/shard_map/ppermute | solution.py:248
  3.7 2.4 %shard_map.110 = (f32[8,256,128]{2,1,0:T(8,128)S(1)}, bf16[8,256,128]{2,1,0:T(8,128)(2,1)S(1)}, bf16[128,1024]{1,0:T(8,128)(2,1)S(1)}, f32[8,128,256]{2,1,0:T(8,...) custom-call(s32[1]{0:T(128)} %bitcast.2.first_ref, ...), custom_call_target="tpu_custom_call" | custom-call | tf_op jit(solution)/shard_map/pallas_call | solution.py:209
  6.1 4.1 %collective-permute-done.k2_ref.got_ref = bf16[128,1024]{1,0:T(8,128)(2,1)S(1)} collective-permute-done((bf16[128,1024]{1,0:T(8,128)(2,1)}, bf16[128,1024]{1,0:T(8,128)(2,1)S(1)}, u32[]{:S(2)}, u32[]{:S(2)}) %collective-permute-start) | collective-permute-done | bytes 262176 | tf_op jit(solution)/shard_map/ppermute | solution.py:248
  10.3 1.8 %collective-permute-start.1 = (bf16[128,1024]{1,0:T(8,128)(2,1)S(1)}, bf16[128,1024]{1,0:T(8,128)(2,1)S(1)}, u32[]{:S(2)}, u32[]{:S(2)}) collective-permute-start(bf16[128,1024]{1,0:T(8,128)(2,1)S(1)} %shard_map.112), channel_id=1, source_target_pairs={{0,8},{8,0},{16,24},{24,16},{1,9},{9,1},{17,25},{25,17},{2,10},{10... | collective-permute-start | bytes 786440 | tf_op jit(solution)/shard_map/ppermute | solution.py:262
  12.0 0.3 collective-permute-start.2
  12.3 1.7 %collective-permute-start.3 = (bf16[128,1024]{1,0:T(8,128)(2,1)}, bf16[128,1024]{1,0:T(8,128)(2,1)S(1)}, u32[]{:S(2)}, u32[]{:S(2)}) collective-permute-start(bf16[128,1024]{1,0:T(8,128)(2,1)} %bitcast.23), channel_id=1, source_target_pairs={{0,16},{8,24},{16,0},{24,8},{1,17},{9,25},{17,1},{25,9},{2,18},{10... | collective-permute-start | bytes 786440 | tf_op jit(solution)/shard_map/ppermute | solution.py:263
  14.1 0.7 %shard_map.111 = (bf16[128,1024]{1,0:T(8,128)(2,1)S(1)}, f32[8,256,256]{2,1,0:T(8,128)S(1)}, f32[8,1,256]{2,1,0:T(1,128)S(1)}, f32[8,1,256]{2,1,0:T(1,128)S(1)}) custom-call(bf16[8,256,128]{2,1,0:T(8,128)(2,1)S(1)} %get-tuple-element.38.qn_ref, f32[8,128,256]{2,1,0:T(8,128)S(1)} %get-tuple-element.39.s_ref, f32[256,128]{1,0:T(8,128)S(1)} %get-tuple-element.40.bias_ref, ...), custom_call_target="tpu_custom_call" | custom-call | tf_op jit(solution)/shard_map/pallas_call | solution.py:209
  14.8 4.7 %collective-permute-done.1.k1_ref = bf16[128,1024]{1,0:T(8,128)(2,1)S(1)} collective-permute-done((bf16[128,1024]{1,0:T(8,128)(2,1)S(1)}, bf16[128,1024]{1,0:T(8,128)(2,1)S(1)}, u32[]{:S(2)}, u32[]{:S(2)}) %collective-permute-start.1) | collective-permute-done | bytes 262176 | tf_op jit(solution)/shard_map/ppermute | solution.py:262
  19.5 2.2 %shard_map.113 = (bf16[128,1024]{1,0:T(8,128)(2,1)S(1)}, f32[8,384,256]{2,1,0:T(8,128)S(1)}, bf16[8,128,256]{2,1,0:T(8,128)(2,1)S(1)}, bf16[128,1024]{1,0:T(8,128)(2,1)S(1)}, bf16[128,1024]{1,0:T(8,128)(2,1)S(1)}) custom-call(bf16[8,256,128]{2,1,0:T(8,128)(2,1)S(1)} %get-tuple-element.38.qn_ref, f32[8,256,256]{2,1,0:T(8,128)S(1)} %get-tuple-element.42.e_ref, ...), custom_call_target="tpu_custom_call" | custom-call | tf_op jit(solution)/shard_map/pallas_call | solution.py:209
  21.7 2.7 %collective-permute-done.2.v1_ref = bf16[128,1024]{1,0:T(8,128)(2,1)S(1)} collective-permute-done((bf16[128,1024]{1,0:T(8,128)(2,1)}, bf16[128,1024]{1,0:T(8,128)(2,1)S(1)}, u32[]{:S(2)}, u32[]{:S(2)}) %collective-permute-start.2) | collective-permute-done | bytes 262176 | tf_op jit(solution)/shard_map/ppermute | solution.py:264
  24.4 0.7 %collective-permute-done.3.v2_ref = bf16[128,1024]{1,0:T(8,128)(2,1)S(1)} collective-permute-done((bf16[128,1024]{1,0:T(8,128)(2,1)}, bf16[128,1024]{1,0:T(8,128)(2,1)S(1)}, u32[]{:S(2)}, u32[]{:S(2)}) %collective-permute-start.3) | collective-permute-done | bytes 262176 | tf_op jit(solution)/shard_map/ppermute | solution.py:263
  25.1 3.0 %shard_map.114 = (bf16[128,1024]{1,0:T(8,128)(2,1)S(1)}, bf16[128,1024]{1,0:T(8,128)(2,1)S(1)}, bf16[8,128,256]{2,1,0:T(8,128)(2,1)S(1)}, f32[8,256,128]{2,1,0:T(8,128)S(1)}, f32[32,2,128]{2,1,0:T(2,128)S(1)}) custom-call(f32[8,384,256]{2,1,0:T(8,128)S(1)} %get-tuple-element.48.p_ref, bf16[8,128,256]{2,1,0:T(8,128)(2,1)S(1)} %get-tuple-element.47.low_ref, ...), custom_call_target="tpu_custom_call" | custom-call | tf_op jit(solution)/shard_map/pallas_call | solution.py:209
  28.1 0.1 collective-permute-start.6
  28.2 2.9 %collective-permute-start.4 = (bf16[128,1024]{1,0:T(8,128)(2,1)S(1)}, bf16[128,1024]{1,0:T(8,128)(2,1)S(1)}, u32[]{:S(2)}, u32[]{:S(2)}) collective-permute-start(bf16[128,1024]{1,0:T(8,128)(2,1)S(1)} %get-tuple-element.59), channel_id=1, source_target_pairs={{0,24},{8,0},{16,8},{24,16},{1,25},{9,1},{17,9},{25,17},{2,26},{10... | collective-permute-start | bytes 786440 | tf_op jit(solution)/shard_map/ppermute | solution.py:282
  31.1 0.6 %collective-permute-start.5 = (bf16[128,1024]{1,0:T(8,128)(2,1)S(1)}, bf16[128,1024]{1,0:T(8,128)(2,1)S(1)}, u32[]{:S(2)}, u32[]{:S(2)}) collective-permute-start(bf16[128,1024]{1,0:T(8,128)(2,1)S(1)} %get-tuple-element.60), channel_id=1, source_target_pairs={{0,16},{8,24},{16,0},{24,8},{1,17},{9,25},{17,1},{25,9},{2,18},{10... | collective-permute-start | bytes 786440 | tf_op jit(solution)/shard_map/ppermute | solution.py:283
  31.7 4.9 %collective-permute-done.6.got_ref.a_ref = bf16[128,1024]{1,0:T(8,128)(2,1)S(1)} collective-permute-done((bf16[128,1024]{1,0:T(8,128)(2,1)S(1)}, bf16[128,1024]{1,0:T(8,128)(2,1)S(1)}, u32[]{:S(2)}, u32[]{:S(2)}) %collective-permute-start.6) | collective-permute-done | bytes 262176 | tf_op jit(solution)/shard_map/ppermute | solution.py:293
  36.6 0.1 shard_map.117
  36.7 0.9 %collective-permute-start.7 = (bf16[128,1024]{1,0:T(8,128)(2,1)S(1)}, bf16[128,1024]{1,0:T(8,128)(2,1)S(1)}, u32[]{:S(2)}, u32[]{:S(2)}) collective-permute-start(bf16[128,1024]{1,0:T(8,128)(2,1)S(1)} %shard_map.117), channel_id=1, source_target_pairs={{0,16},{8,24},{16,0},{24,8},{1,17},{9,25},{17,1},{25,9},{2,18},{10... | collective-permute-start | bytes 786440 | tf_op jit(solution)/shard_map/ppermute | solution.py:295
  37.6 11.6 %all_to_all.5.parts_ref = f32[32,2,128]{2,1,0:T(2,128)S(1)} all-to-all(f32[32,2,128]{2,1,0:T(2,128)S(1)} %get-tuple-element.62), channel_id=1, replica_groups=mesh['ctx'=4,'dp'=8] {'ctx','dp'}, dimensions={0} | all-to-all | bytes 65536 | tf_op jit(solution)/shard_map/all_to_all | solution.py:296
  49.2 1.6 %shard_map.116 = (f32[1,128]{1,0:T(1,128)}, f32[1,128]{1,0:T(1,128)}, f32[128,1024]{1,0:T(8,128)S(1)}, f32[128,1024]{1,0:T(8,128)S(1)}) custom-call(bf16[128,1024]{1,0:T(8,128)(2,1)} %bitcast.19, f32[32,2,128]{2,1,0:T(2,128)S(1)} %all_to_all.5.parts_ref), custom_call_target="tpu_custom_call" | custom-call | tf_op jit(solution)/shard_map/pallas_call | solution.py:209
  50.8 0.7 %copy-done = bf16[128,1024]{1,0:T(8,128)(2,1)} copy-done((bf16[128,1024]{1,0:T(8,128)(2,1)}, bf16[128,1024]{1,0:T(8,128)(2,1)S(1)}, u32[]{:S(2)}) %copy-start) | copy-done | bytes 262168
  51.5 0.1 copy-done.1
  51.6 3.2 %shard_map.115 = (bf16[128,2048]{1,0:T(8,128)(2,1)}, f32[128,1024]{1,0:T(8,128)S(1)}, bf16[128,1024]{1,0:T(8,128)(2,1)}) custom-call(bf16[128,2048]{1,0:T(8,128)(2,1)} %bitcast.14, bf16[128,2048]{1,0:T(8,128)(2,1)} %bitcast.16, bf16[8,128,256]{2,1,0:T(8,128)(2,1)S(1)} %get-tuple-element.47.low_ref, bf16[8,128,256]{2,1,0:T(8,128)(2,1)S(1)} %get-tuple-element.56.ds_ref, ...), custom_call_target="tpu_custom_call" | custom-call | tf_op jit(solution)/shard_map/pallas_call | solution.py:209
  54.9 1.0 %shard_map.118 = bf16[128,1024]{1,0:T(8,128)(2,1)} custom-call(s32[1]{0:T(128)} %bitcast.7.odd_ref, f32[128,1024]{1,0:T(8,128)S(1)} %get-tuple-element.63.kh_ref, f32[128,1024]{1,0:T(8,128)S(1)} %get-tuple-element.64.ki_ref, f32[128,1024]{1,0:T(8,128)S(1)} %get-tuple-element.65.dk_ref, bf16[128,1024]{1,0:T(8,128)(2,1)S(1)} %collective-permute-done.6.got_ref.a_ref, ...), custom_call_target="tpu_custom_call" | custom-call | tf_op jit(solution)/shard_map/pallas_call | solution.py:209
  (6 shorter events, 0.0 us)
Async XLA Ops:
  0.6 9.6 %collective-permute-start = (bf16[128,1024]{1,0:T(8,128)(2,1)}, bf16[128,1024]{1,0:T(8,128)(2,1)S(1)}, u32[]{:S(2)}, u32[]{:S(2)}) collective-permute-start(bf16[128,1024]{1,0:T(8,128)(2,1)} %bitcast.17), channel_id=1, source_target_pairs={{0,16},{8,24},{16,0},{24,8},{1,17},{9,25},{17,1},{25,9},{2,18},{10... | collective-permute-start | bytes 786440 | tf_op jit(solution)/shard_map/ppermute | solution.py:248
  10.3 9.2 %collective-permute-start.1 = (bf16[128,1024]{1,0:T(8,128)(2,1)S(1)}, bf16[128,1024]{1,0:T(8,128)(2,1)S(1)}, u32[]{:S(2)}, u32[]{:S(2)}) collective-permute-start(bf16[128,1024]{1,0:T(8,128)(2,1)S(1)} %shard_map.112), channel_id=1, source_target_pairs={{0,8},{8,0},{16,24},{24,16},{1,9},{9,1},{17,25},{25,17},{2,10},{10... | collective-permute-start | bytes 786440 | tf_op jit(solution)/shard_map/ppermute | solution.py:262
  12.0 12.4 %collective-permute-start.2 = (bf16[128,1024]{1,0:T(8,128)(2,1)}, bf16[128,1024]{1,0:T(8,128)(2,1)S(1)}, u32[]{:S(2)}, u32[]{:S(2)}) collective-permute-start(bf16[128,1024]{1,0:T(8,128)(2,1)} %bitcast.22), channel_id=1, source_target_pairs={{0,8},{8,16},{16,24},{24,0},{1,9},{9,17},{17,25},{25,1},{2,10},{10... | collective-permute-start | bytes 786440 | tf_op jit(solution)/shard_map/ppermute | solution.py:264
  12.3 12.7 %collective-permute-start.3 = (bf16[128,1024]{1,0:T(8,128)(2,1)}, bf16[128,1024]{1,0:T(8,128)(2,1)S(1)}, u32[]{:S(2)}, u32[]{:S(2)}) collective-permute-start(bf16[128,1024]{1,0:T(8,128)(2,1)} %bitcast.23), channel_id=1, source_target_pairs={{0,16},{8,24},{16,0},{24,8},{1,17},{9,25},{17,1},{25,9},{2,18},{10... | collective-permute-start | bytes 786440 | tf_op jit(solution)/shard_map/ppermute | solution.py:263
  28.1 8.5 %collective-permute-start.6 = (bf16[128,1024]{1,0:T(8,128)(2,1)S(1)}, bf16[128,1024]{1,0:T(8,128)(2,1)S(1)}, u32[]{:S(2)}, u32[]{:S(2)}) collective-permute-start(bf16[128,1024]{1,0:T(8,128)(2,1)S(1)} %get-tuple-element.66), channel_id=1, source_target_pairs={{0,8},{8,0},{16,24},{24,16},{1,9},{9,1},{17,25},{25,17},{2,10},{10... | collective-permute-start | bytes 786440 | tf_op jit(solution)/shard_map/ppermute | solution.py:293
  28.2 22.6 %collective-permute-start.4 = (bf16[128,1024]{1,0:T(8,128)(2,1)S(1)}, bf16[128,1024]{1,0:T(8,128)(2,1)S(1)}, u32[]{:S(2)}, u32[]{:S(2)}) collective-permute-start(bf16[128,1024]{1,0:T(8,128)(2,1)S(1)} %get-tuple-element.59), channel_id=1, source_target_pairs={{0,24},{8,0},{16,8},{24,16},{1,25},{9,1},{17,9},{25,17},{2,26},{10... | collective-permute-start | bytes 786440 | tf_op jit(solution)/shard_map/ppermute | solution.py:282
  31.1 19.7 %collective-permute-start.5 = (bf16[128,1024]{1,0:T(8,128)(2,1)S(1)}, bf16[128,1024]{1,0:T(8,128)(2,1)S(1)}, u32[]{:S(2)}, u32[]{:S(2)}) collective-permute-start(bf16[128,1024]{1,0:T(8,128)(2,1)S(1)} %get-tuple-element.60), channel_id=1, source_target_pairs={{0,16},{8,24},{16,0},{24,8},{1,17},{9,25},{17,1},{25,9},{2,18},{10... | collective-permute-start | bytes 786440 | tf_op jit(solution)/shard_map/ppermute | solution.py:283
  36.7 18.2 %collective-permute-start.7 = (bf16[128,1024]{1,0:T(8,128)(2,1)S(1)}, bf16[128,1024]{1,0:T(8,128)(2,1)S(1)}, u32[]{:S(2)}, u32[]{:S(2)}) collective-permute-start(bf16[128,1024]{1,0:T(8,128)(2,1)S(1)} %shard_map.117), channel_id=1, source_target_pairs={{0,16},{8,24},{16,0},{24,8},{1,17},{9,25},{17,1},{25,9},{2,18},{10... | collective-permute-start | bytes 786440 | tf_op jit(solution)/shard_map/ppermute | solution.py:295
  50.8 0.7 %copy-start = (bf16[128,1024]{1,0:T(8,128)(2,1)}, bf16[128,1024]{1,0:T(8,128)(2,1)S(1)}, u32[]{:S(2)}) copy-start(bf16[128,1024]{1,0:T(8,128)(2,1)S(1)} %collective-permute-done.4.a_ref) | copy-start | bytes 786436
  50.8 0.8 %copy-start.1 = (bf16[128,1024]{1,0:T(8,128)(2,1)}, bf16[128,1024]{1,0:T(8,128)(2,1)S(1)}, u32[]{:S(2)}) copy-start(bf16[128,1024]{1,0:T(8,128)(2,1)S(1)} %collective-permute-done.5.b_ref) | copy-start | bytes 786436

commit v3 on v2

--- a/solution.py
+++ b/solution.py
@@ -109,25 +109,31 @@
 def weigh_kernel(qn_ref, e_ref, top_ref, sum_ref, bias_ref, k1_ref, go_ref, kg_ref, kn_ref, p_ref, low_ref, g1v_ref, g2v_ref):
     rows = k1_ref.shape[0]
     bias = jnp.concatenate([bias_ref[rows:]] * GROUP, axis=1)
-    for u in range(KEY_VALUE_HEADS):
-        k = k1_ref[:, columns(u)].astype(F32)
-        kn = (k * inverse_rms(k) * kg_ref[...]).astype(BF16)
-        kn_ref[:, columns(u)] = kn
-        s1 = dot(kn, qn_ref[u], 1, 1) * (score_scale * LOG2E) + bias
-        top = jnp.maximum(top_ref[u], jnp.max(s1, axis=0, keepdims=True))
-        e1 = jnp.exp2(s1 - top)
-        fade = jnp.exp2(top_ref[u] - top)
-        inv = 1.0 / (sum_ref[u] * fade + jnp.sum(e1, axis=0, keepdims=True))
-        fade = fade * inv
-        p2 = e_ref[u, :rows] * fade
-        p1 = e1 * inv
-        p_ref[u, :rows] = p2
-        p_ref[u, rows:WINDOW_SIZE] = p1
-        p0 = e_ref[u, rows:] * fade
-        p_ref[u, WINDOW_SIZE:] = p0
-        low_ref[u] = p0.astype(BF16)
-        g1v_ref[:, columns(u)] = dot(p1.astype(BF16), go_ref[u], 1, 0).astype(BF16)
-        g2v_ref[:, columns(u)] = dot(p2.astype(BF16), go_ref[u], 1, 0).astype(BF16)
+    ready = {}
+    for turn in range(KEY_VALUE_HEADS + 2):
+        u = turn
+        if u < KEY_VALUE_HEADS:
+            k = k1_ref[:, columns(u)].astype(F32)
+            kn = (k * inverse_rms(k) * kg_ref[...]).astype(BF16)
+            kn_ref[:, columns(u)] = kn
+            ready[u] = dot(kn, qn_ref[u], 1, 1) * (score_scale * LOG2E) + bias
+        u = turn - 2
+        if u >= 0:
+            s1 = ready.pop(u)
+            top = jnp.maximum(top_ref[u], jnp.max(s1, axis=0, keepdims=True))
+            e1 = jnp.exp2(s1 - top)
+            fade = jnp.exp2(top_ref[u] - top)
+            inv = 1.0 / (sum_ref[u] * fade + jnp.sum(e1, axis=0, keepdims=True))
+            fade = fade * inv
+            p2 = e_ref[u, :rows] * fade
+            p1 = e1 * inv
+            p0 = e_ref[u, rows:] * fade
+            p_ref[u, :rows] = p2
+            p_ref[u, rows:WINDOW_SIZE] = p1
+            p_ref[u, WINDOW_SIZE:] = p0
+            low_ref[u] = p0.astype(BF16)
+            g1v_ref[:, columns(u)] = dot(p1.astype(BF16), go_ref[u], 1, 0).astype(BF16)
+            g2v_ref[:, columns(u)] = dot(p2.astype(BF16), go_ref[u], 1, 0).astype(BF16)
 
 
 def score_kernel(p_ref, low_ref, v0_ref, v1_ref, v2_ref, go_ref, got_ref, dp_ref, qh_ref, qn_ref, kn2_ref, kn1_ref, kn0_ref,
@@ -135,24 +141,31 @@
     rows = v0_ref.shape[0]
     q_part = jnp.zeros((1, HEAD_SIZE), F32)
     k_part = jnp.zeros((1, HEAD_SIZE), F32)
-    for u in range(KEY_VALUE_HEADS):
-        v = jnp.concatenate([v2_ref[:, columns(u)], v1_ref[:, columns(u)]], axis=0)
-        qn = qn_ref[u]
-        p, p0 = p_ref[u, :WINDOW_SIZE], p_ref[u, WINDOW_SIZE:]
-        attended = dot(v, p.astype(BF16), 0, 0) + dot(v0_ref[:, columns(u)], low_ref[u], 0, 0)
-        attended = attended.astype(BF16).astype(F32)
-        delta = jnp.sum(got_ref[u].astype(F32) * attended, axis=0, keepdims=True)
-        ds = (p * (dot(v, go_ref[u], 1, 1) - delta)).astype(BF16)
-        ds0 = (p0 * (dp_ref[u] - delta)).astype(BF16)
-        ds_ref[u] = ds0
-        g = (dot(ds, qn, 1, 0) * score_scale).astype(BF16)
-        g2k_ref[:, columns(u)] = g[:rows]
-        g1k_ref[:, columns(u)] = g[rows:]
-        kn = jnp.concatenate([ref[:, columns(u)] for ref in (kn2_ref, kn1_ref, kn0_ref)], axis=0)
-        dqn = dot(jnp.concatenate([ds, ds0], axis=0), kn, 0, 0) * score_scale
-        dqn_ref[u] = dqn
-        q_part = q_part + jnp.sum(dqn * qh_ref[u], axis=0, keepdims=True)
-        k_part = k_part + jnp.sum(dqn * qn.astype(F32), axis=0, keepdims=True)
+    ready = {}
+    for turn in range(KEY_VALUE_HEADS + 2):
+        u = turn
+        if u < KEY_VALUE_HEADS:
+            v = jnp.concatenate([v2_ref[:, columns(u)], v1_ref[:, columns(u)]], axis=0)
+            p, p0 = p_ref[u, :WINDOW_SIZE], p_ref[u, WINDOW_SIZE:]
+            attended = dot(v, p.astype(BF16), 0, 0) + dot(v0_ref[:, columns(u)], low_ref[u], 0, 0)
+            attended = attended.astype(BF16).astype(F32)
+            delta = jnp.sum(got_ref[u].astype(F32) * attended, axis=0, keepdims=True)
+            ds = (p * (dot(v, go_ref[u], 1, 1) - delta)).astype(BF16)
+            ds0 = (p0 * (dp_ref[u] - delta)).astype(BF16)
+            ds_ref[u] = ds0
+            ready[u] = (ds, ds0)
+        u = turn - 2
+        if u >= 0:
+            ds, ds0 = ready.pop(u)
+            qn = qn_ref[u]
+            g = (dot(ds, qn, 1, 0) * score_scale).astype(BF16)
+            g2k_ref[:, columns(u)] = g[:rows]
+            g1k_ref[:, columns(u)] = g[rows:]
+            kn = jnp.concatenate([ref[:, columns(u)] for ref in (kn2_ref, kn1_ref, kn0_ref)], axis=0)
+            dqn = jnp.transpose(dot(kn, jnp.concatenate([ds, ds0], axis=0), 0, 0)) * score_scale
+            dqn_ref[u] = dqn
+            q_part = q_part + jnp.sum(dqn * qh_ref[u], axis=0, keepdims=True)
+            k_part = k_part + jnp.sum(dqn * qn.astype(F32), axis=0, keepdims=True)
     parts = jnp.concatenate([q_part, k_part / kg_ref[...]], axis=0)
     gains_ref[...] = jnp.broadcast_to(parts[None], gains_ref.shape)
 
@@ -261,7 +274,7 @@
     turned = call(turn_kernel, [held(flat, BF16)], near(k0, k2), (parity,))[0]
     k1 = lax.ppermute(turned, "ctx", swap)
     v2 = lax.ppermute(v, "ctx", ahead)
-    v1 = lax.ppermute(v, "ctx", follow)
+    v1 = lax.ppermute(v, "ctx", follow[:-1])
 
     kn2, e, top, norm = call(
         early_kernel,
@@ -279,7 +292,7 @@
         ],
         near(qn, e, top, norm, bias, k1, go2, kg),
     )
-    av = lax.ppermute(g1v, "ctx", lead)
+    av = lax.ppermute(g1v, "ctx", lead[1:])
     bv = lax.ppermute(g2v, "ctx", behind)
 
     g1k, g2k, ds0, dqn, gains = call(

time: 56.1 us -> 57.7 us (1.029)
  starting transfers between devices: 11.3 us -> 16.8 us
  Pallas kernels: 14.3 us -> 12.1 us
  waiting for transfers between devices: 17.1 us -> 16 us
  blocking collectives: 11.6 us -> 11 us
    ppermute x1, starting transfers between devices: 0.57 us -> 4.14 us  [per_device(): bv = lax.ppermute(g2v, 'ctx', behind)]
    ppermute x1, waiting for transfers between devices: 0.68 us -> 3.68 us  [per_device(): v2 = lax.ppermute(v, 'ctx', ahead)]
    ppermute x1, waiting for transfers between devices: 4.69 us -> 2.43 us  [per_device(): k1 = lax.ppermute(turned, 'ctx', swap)]
    pallas_call x9, Pallas kernels: 14.3 us -> 12.1 us  [call(): pl.pallas_call(kernel, in_specs=[pl.BlockSpec(memory_space=pltpu.SMEM)] *...]
    ppermute x1, starting transfers between devices: 0.91 us -> 2.44 us  [per_device(): bk = lax.ppermute(joined, 'ctx', behind)]
    ppermute x1, waiting for transfers between devices: 4.92 us -> 3.72 us  [per_device(): ak = lax.ppermute(g1k, 'ctx', swap)]
    ppermute x2, waiting for transfers between devices: 2.7 us -> 2.05 us  [the longest x1 2.05 us: per_device(): v1 = lax.ppermute(v, 'ctx', follow[:-1])]
    all_to_all x1, blocking collectives: 11.6 us -> 11 us  [per_device(): spread = lax.all_to_all(gains, ('ctx', 'dp'), 0, 0)]
  transfers between devices with their start and end apart: 8 -> 8, of which waited for: 5 -> 5; matrix products, arithmetic and copies ran while one was open for 0% -> 0% of each run, Pallas kernels for 18% -> 16%
where the time goes in v3:
time: 57.7 us; the launch traced here: 57.4 us
  starting transfers between devices  16.8 us (29%)
  waiting for transfers between devices  16 us (28%)
  Pallas kernels  12.1 us (21%)
  blocking collectives  11 us (19%)
  local copies, waits for them, and re-layouts  0.77 us (1%)
  between operations  0.7 us (1%)
    pallas_call x9, Pallas kernels, call(): pl.pallas_call(kernel, in_specs=[pl.BlockSpec(memory_space=pltpu.SMEM)] *...  12.1 us
    all_to_all x1, blocking collectives, per_device(): spread = lax.all_to_all(gains, ('ctx', 'dp'), 0, 0)  11 us
    ppermute x1, starting transfers between devices, per_device(): bv = lax.ppermute(g2v, 'ctx', behind)  4.14 us
    ppermute x1, waiting for transfers between devices, per_device(): k2 = lax.ppermute(k, 'ctx', ahead)  4.13 us
    ppermute x1, waiting for transfers between devices, per_device(): ak = lax.ppermute(g1k, 'ctx', swap)  3.72 us
    ppermute x1, waiting for transfers between devices, per_device(): v2 = lax.ppermute(v, 'ctx', ahead)  3.68 us
    ppermute x1, starting transfers between devices, per_device(): k2 = lax.ppermute(k, 'ctx', ahead)  3.06 us
    ppermute x1, starting transfers between devices, per_device(): bk = lax.ppermute(joined, 'ctx', behind)  2.44 us
  transfers between devices with their start and end apart: 8, of which 5 were waited for; matrix products, arithmetic and copies ran while one was open for 0% of the time, Pallas kernels for 16%

profile of v3, /device:TPU:0, one launch (start us, length us, event | category | flops | bytes accessed | tf_op | source)
XLA Modules:
  0.0 57.4 jit_solution(17072059644989698595)
XLA Ops:
  0.6 3.1 %collective-permute-start = (bf16[128,1024]{1,0:T(8,128)(2,1)}, bf16[128,1024]{1,0:T(8,128)(2,1)S(1)}, u32[]{:S(2)}, u32[]{:S(2)}) collective-permute-start(bf16[128,1024]{1,0:T(8,128)(2,1)} %bitcast.17), channel_id=1, source_target_pairs={{0,16},{8,24},{16,0},{24,8},{1,17},{9,25},{17,1},{25,9},{2,18},{10... | collective-permute-start | bytes 786440 | tf_op jit(solution)/shard_map/ppermute | solution.py:261
  3.7 2.4 %shard_map.110 = (f32[8,256,128]{2,1,0:T(8,128)S(1)}, bf16[8,256,128]{2,1,0:T(8,128)(2,1)S(1)}, bf16[128,1024]{1,0:T(8,128)(2,1)S(1)}, f32[8,128,256]{2,1,0:T(8,...) custom-call(s32[1]{0:T(128)} %bitcast.2.first_ref, ...), custom_call_target="tpu_custom_call" | custom-call | tf_op jit(solution)/shard_map/pallas_call | solution.py:222
  6.1 4.1 %collective-permute-done.k2_ref.got_ref = bf16[128,1024]{1,0:T(8,128)(2,1)S(1)} collective-permute-done((bf16[128,1024]{1,0:T(8,128)(2,1)}, bf16[128,1024]{1,0:T(8,128)(2,1)S(1)}, u32[]{:S(2)}, u32[]{:S(2)}) %collective-permute-start) | collective-permute-done | bytes 262176 | tf_op jit(solution)/shard_map/ppermute | solution.py:261
  10.3 1.8 %collective-permute-start.1 = (bf16[128,1024]{1,0:T(8,128)(2,1)S(1)}, bf16[128,1024]{1,0:T(8,128)(2,1)S(1)}, u32[]{:S(2)}, u32[]{:S(2)}) collective-permute-start(bf16[128,1024]{1,0:T(8,128)(2,1)S(1)} %shard_map.112), channel_id=1, source_target_pairs={{0,8},{8,0},{16,24},{24,16},{1,9},{9,1},{17,25},{25,17},{2,10},{10... | collective-permute-start | bytes 786440 | tf_op jit(solution)/shard_map/ppermute | solution.py:275
  12.0 2.2 %collective-permute-start.2 = (bf16[128,1024]{1,0:T(8,128)(2,1)}, bf16[128,1024]{1,0:T(8,128)(2,1)S(1)}, u32[]{:S(2)}, u32[]{:S(2)}) collective-permute-start(bf16[128,1024]{1,0:T(8,128)(2,1)} %bitcast.22), channel_id=1, source_target_pairs={{0,8},{8,16},{16,24},{1,9},{9,17},{17,25},{2,10},{10,18},{18,26},{... | collective-permute-start | bytes 786440 | tf_op jit(solution)/shard_map/ppermute | solution.py:277
  14.3 1.8 %collective-permute-start.3 = (bf16[128,1024]{1,0:T(8,128)(2,1)}, bf16[128,1024]{1,0:T(8,128)(2,1)S(1)}, u32[]{:S(2)}, u32[]{:S(2)}) collective-permute-start(bf16[128,1024]{1,0:T(8,128)(2,1)} %bitcast.23), channel_id=1, source_target_pairs={{0,16},{8,24},{16,0},{24,8},{1,17},{9,25},{17,1},{25,9},{2,18},{10... | collective-permute-start | bytes 786440 | tf_op jit(solution)/shard_map/ppermute | solution.py:276
  16.1 0.7 %shard_map.111 = (bf16[128,1024]{1,0:T(8,128)(2,1)S(1)}, f32[8,256,256]{2,1,0:T(8,128)S(1)}, f32[8,1,256]{2,1,0:T(1,128)S(1)}, f32[8,1,256]{2,1,0:T(1,128)S(1)}) custom-call(bf16[8,256,128]{2,1,0:T(8,128)(2,1)S(1)} %get-tuple-element.38.qn_ref, f32[8,128,256]{2,1,0:T(8,128)S(1)} %get-tuple-element.39.s_ref, f32[256,128]{1,0:T(8,128)S(1)} %get-tuple-element.40.bias_ref, ...), custom_call_target="tpu_custom_call" | custom-call | tf_op jit(solution)/shard_map/pallas_call | solution.py:222
  16.8 2.4 %collective-permute-done.1.k1_ref = bf16[128,1024]{1,0:T(8,128)(2,1)S(1)} collective-permute-done((bf16[128,1024]{1,0:T(8,128)(2,1)S(1)}, bf16[128,1024]{1,0:T(8,128)(2,1)S(1)}, u32[]{:S(2)}, u32[]{:S(2)}) %collective-permute-start.1) | collective-permute-done | bytes 262176 | tf_op jit(solution)/shard_map/ppermute | solution.py:275
  19.2 1.2 %shard_map.113 = (bf16[128,1024]{1,0:T(8,128)(2,1)S(1)}, f32[8,384,256]{2,1,0:T(8,128)S(1)}, bf16[8,128,256]{2,1,0:T(8,128)(2,1)S(1)}, bf16[128,1024]{1,0:T(8,128)(2,1)S(1)}, bf16[128,1024]{1,0:T(8,128)(2,1)S(1)}) custom-call(bf16[8,256,128]{2,1,0:T(8,128)(2,1)S(1)} %get-tuple-element.38.qn_ref, f32[8,256,256]{2,1,0:T(8,128)S(1)} %get-tuple-element.42.e_ref, ...), custom_call_target="tpu_custom_call" | custom-call | tf_op jit(solution)/shard_map/pallas_call | solution.py:222
  20.4 2.0 %collective-permute-done.2.v1_ref = bf16[128,1024]{1,0:T(8,128)(2,1)S(1)} collective-permute-done((bf16[128,1024]{1,0:T(8,128)(2,1)}, bf16[128,1024]{1,0:T(8,128)(2,1)S(1)}, u32[]{:S(2)}, u32[]{:S(2)}) %collective-permute-start.2) | collective-permute-done | bytes 262176 | tf_op jit(solution)/shard_map/ppermute | solution.py:277
  22.5 3.7 %collective-permute-done.3.v2_ref = bf16[128,1024]{1,0:T(8,128)(2,1)S(1)} collective-permute-done((bf16[128,1024]{1,0:T(8,128)(2,1)}, bf16[128,1024]{1,0:T(8,128)(2,1)S(1)}, u32[]{:S(2)}, u32[]{:S(2)}) %collective-permute-start.3) | collective-permute-done | bytes 262176 | tf_op jit(solution)/shard_map/ppermute | solution.py:276
  26.1 1.8 %shard_map.114 = (bf16[128,1024]{1,0:T(8,128)(2,1)S(1)}, bf16[128,1024]{1,0:T(8,128)(2,1)S(1)}, bf16[8,128,256]{2,1,0:T(8,128)(2,1)S(1)}, f32[8,256,128]{2,1,0:T(8,128)S(1)}, f32[32,2,128]{2,1,0:T(2,128)S(1)}) custom-call(f32[8,384,256]{2,1,0:T(8,128)S(1)} %get-tuple-element.48.p_ref, bf16[8,128,256]{2,1,0:T(8,128)(2,1)S(1)} %get-tuple-element.47.low_ref, ...), custom_call_target="tpu_custom_call" | custom-call | tf_op jit(solution)/shard_map/pallas_call | solution.py:222
  28.0 0.1 collective-permute-start.6
  28.1 1.3 %collective-permute-start.4 = (bf16[128,1024]{1,0:T(8,128)(2,1)S(1)}, bf16[128,1024]{1,0:T(8,128)(2,1)S(1)}, u32[]{:S(2)}, u32[]{:S(2)}) collective-permute-start(bf16[128,1024]{1,0:T(8,128)(2,1)S(1)} %get-tuple-element.59), channel_id=1, source_target_pairs={{8,0},{16,8},{24,16},{9,1},{17,9},{25,17},{10,2},{18,10},{26,18},{... | collective-permute-start | bytes 786440 | tf_op jit(solution)/shard_map/ppermute | solution.py:295
  29.4 4.1 %collective-permute-start.5 = (bf16[128,1024]{1,0:T(8,128)(2,1)S(1)}, bf16[128,1024]{1,0:T(8,128)(2,1)S(1)}, u32[]{:S(2)}, u32[]{:S(2)}) collective-permute-start(bf16[128,1024]{1,0:T(8,128)(2,1)S(1)} %get-tuple-element.60), channel_id=1, source_target_pairs={{0,16},{8,24},{16,0},{24,8},{1,17},{9,25},{17,1},{25,9},{2,18},{10... | collective-permute-start | bytes 786440 | tf_op jit(solution)/shard_map/ppermute | solution.py:296
  33.5 3.7 %collective-permute-done.6.got_ref.a_ref = bf16[128,1024]{1,0:T(8,128)(2,1)S(1)} collective-permute-done((bf16[128,1024]{1,0:T(8,128)(2,1)S(1)}, bf16[128,1024]{1,0:T(8,128)(2,1)S(1)}, u32[]{:S(2)}, u32[]{:S(2)}) %collective-permute-start.6) | collective-permute-done | bytes 262176 | tf_op jit(solution)/shard_map/ppermute | solution.py:306
  37.2 0.1 shard_map.117
  37.3 2.4 %collective-permute-start.7 = (bf16[128,1024]{1,0:T(8,128)(2,1)S(1)}, bf16[128,1024]{1,0:T(8,128)(2,1)S(1)}, u32[]{:S(2)}, u32[]{:S(2)}) collective-permute-start(bf16[128,1024]{1,0:T(8,128)(2,1)S(1)} %shard_map.117), channel_id=1, source_target_pairs={{0,16},{8,24},{16,0},{24,8},{1,17},{9,25},{17,1},{25,9},{2,18},{10... | collective-permute-start | bytes 786440 | tf_op jit(solution)/shard_map/ppermute | solution.py:308
  39.8 11.0 %all_to_all.5.parts_ref = f32[32,2,128]{2,1,0:T(2,128)S(1)} all-to-all(f32[32,2,128]{2,1,0:T(2,128)S(1)} %get-tuple-element.62), channel_id=1, replica_groups=mesh['ctx'=4,'dp'=8] {'ctx','dp'}, dimensions={0} | all-to-all | bytes 65536 | tf_op jit(solution)/shard_map/all_to_all | solution.py:309
  50.8 1.6 %shard_map.116 = (f32[1,128]{1,0:T(1,128)}, f32[1,128]{1,0:T(1,128)}, f32[128,1024]{1,0:T(8,128)S(1)}, f32[128,1024]{1,0:T(8,128)S(1)}) custom-call(bf16[128,1024]{1,0:T(8,128)(2,1)} %bitcast.19, f32[32,2,128]{2,1,0:T(2,128)S(1)} %all_to_all.5.parts_ref), custom_call_target="tpu_custom_call" | custom-call | tf_op jit(solution)/shard_map/pallas_call | solution.py:222
  52.4 0.7 %copy-done = bf16[128,1024]{1,0:T(8,128)(2,1)} copy-done((bf16[128,1024]{1,0:T(8,128)(2,1)}, bf16[128,1024]{1,0:T(8,128)(2,1)S(1)}, u32[]{:S(2)}) %copy-start) | copy-done | bytes 262168
  53.1 0.1 copy-done.1
  53.2 3.2 %shard_map.115 = (bf16[128,2048]{1,0:T(8,128)(2,1)}, f32[128,1024]{1,0:T(8,128)S(1)}, bf16[128,1024]{1,0:T(8,128)(2,1)}) custom-call(bf16[128,2048]{1,0:T(8,128)(2,1)} %bitcast.14, bf16[128,2048]{1,0:T(8,128)(2,1)} %bitcast.16, bf16[8,128,256]{2,1,0:T(8,128)(2,1)S(1)} %get-tuple-element.47.low_ref, bf16[8,128,256]{2,1,0:T(8,128)(2,1)S(1)} %get-tuple-element.56.ds_ref, ...), custom_call_target="tpu_custom_call" | custom-call | tf_op jit(solution)/shard_map/pallas_call | solution.py:222
  56.4 1.0 %shard_map.118 = bf16[128,1024]{1,0:T(8,128)(2,1)} custom-call(s32[1]{0:T(128)} %bitcast.7.odd_ref, f32[128,1024]{1,0:T(8,128)S(1)} %get-tuple-element.63.kh_ref, f32[128,1024]{1,0:T(8,128)S(1)} %get-tuple-element.64.ki_ref, f32[128,1024]{1,0:T(8,128)S(1)} %get-tuple-element.65.dk_ref, bf16[128,1024]{1,0:T(8,128)(2,1)S(1)} %collective-permute-done.6.got_ref.a_ref, ...), custom_call_target="tpu_custom_call" | custom-call | tf_op jit(solution)/shard_map/pallas_call | solution.py:222
  (6 shorter events, 0.0 us)
Async XLA Ops:
  0.6 9.6 %collective-permute-start = (bf16[128,1024]{1,0:T(8,128)(2,1)}, bf16[128,1024]{1,0:T(8,128)(2,1)S(1)}, u32[]{:S(2)}, u32[]{:S(2)}) collective-permute-start(bf16[128,1024]{1,0:T(8,128)(2,1)} %bitcast.17), channel_id=1, source_target_pairs={{0,16},{8,24},{16,0},{24,8},{1,17},{9,25},{17,1},{25,9},{2,18},{10... | collective-permute-start | bytes 786440 | tf_op jit(solution)/shard_map/ppermute | solution.py:261
  10.3 9.0 %collective-permute-start.1 = (bf16[128,1024]{1,0:T(8,128)(2,1)S(1)}, bf16[128,1024]{1,0:T(8,128)(2,1)S(1)}, u32[]{:S(2)}, u32[]{:S(2)}) collective-permute-start(bf16[128,1024]{1,0:T(8,128)(2,1)S(1)} %shard_map.112), channel_id=1, source_target_pairs={{0,8},{8,0},{16,24},{24,16},{1,9},{9,1},{17,25},{25,17},{2,10},{10... | collective-permute-start | bytes 786440 | tf_op jit(solution)/shard_map/ppermute | solution.py:275
  12.0 10.4 %collective-permute-start.2 = (bf16[128,1024]{1,0:T(8,128)(2,1)}, bf16[128,1024]{1,0:T(8,128)(2,1)S(1)}, u32[]{:S(2)}, u32[]{:S(2)}) collective-permute-start(bf16[128,1024]{1,0:T(8,128)(2,1)} %bitcast.22), channel_id=1, source_target_pairs={{0,8},{8,16},{16,24},{1,9},{9,17},{17,25},{2,10},{10,18},{18,26},{... | collective-permute-start | bytes 786440 | tf_op jit(solution)/shard_map/ppermute | solution.py:277
  14.3 11.9 %collective-permute-start.3 = (bf16[128,1024]{1,0:T(8,128)(2,1)}, bf16[128,1024]{1,0:T(8,128)(2,1)S(1)}, u32[]{:S(2)}, u32[]{:S(2)}) collective-permute-start(bf16[128,1024]{1,0:T(8,128)(2,1)} %bitcast.23), channel_id=1, source_target_pairs={{0,16},{8,24},{16,0},{24,8},{1,17},{9,25},{17,1},{25,9},{2,18},{10... | collective-permute-start | bytes 786440 | tf_op jit(solution)/shard_map/ppermute | solution.py:276
  28.0 9.2 %collective-permute-start.6 = (bf16[128,1024]{1,0:T(8,128)(2,1)S(1)}, bf16[128,1024]{1,0:T(8,128)(2,1)S(1)}, u32[]{:S(2)}, u32[]{:S(2)}) collective-permute-start(bf16[128,1024]{1,0:T(8,128)(2,1)S(1)} %get-tuple-element.66), channel_id=1, source_target_pairs={{0,8},{8,0},{16,24},{24,16},{1,9},{9,1},{17,25},{25,17},{2,10},{10... | collective-permute-start | bytes 786440 | tf_op jit(solution)/shard_map/ppermute | solution.py:306
  28.1 24.3 %collective-permute-start.4 = (bf16[128,1024]{1,0:T(8,128)(2,1)S(1)}, bf16[128,1024]{1,0:T(8,128)(2,1)S(1)}, u32[]{:S(2)}, u32[]{:S(2)}) collective-permute-start(bf16[128,1024]{1,0:T(8,128)(2,1)S(1)} %get-tuple-element.59), channel_id=1, source_target_pairs={{8,0},{16,8},{24,16},{9,1},{17,9},{25,17},{10,2},{18,10},{26,18},{... | collective-permute-start | bytes 786440 | tf_op jit(solution)/shard_map/ppermute | solution.py:295
  29.4 23.0 %collective-permute-start.5 = (bf16[128,1024]{1,0:T(8,128)(2,1)S(1)}, bf16[128,1024]{1,0:T(8,128)(2,1)S(1)}, u32[]{:S(2)}, u32[]{:S(2)}) collective-permute-start(bf16[128,1024]{1,0:T(8,128)(2,1)S(1)} %get-tuple-element.60), channel_id=1, source_target_pairs={{0,16},{8,24},{16,0},{24,8},{1,17},{9,25},{17,1},{25,9},{2,18},{10... | collective-permute-start | bytes 786440 | tf_op jit(solution)/shard_map/ppermute | solution.py:296
  37.3 19.1 %collective-permute-start.7 = (bf16[128,1024]{1,0:T(8,128)(2,1)S(1)}, bf16[128,1024]{1,0:T(8,128)(2,1)S(1)}, u32[]{:S(2)}, u32[]{:S(2)}) collective-permute-start(bf16[128,1024]{1,0:T(8,128)(2,1)S(1)} %shard_map.117), channel_id=1, source_target_pairs={{0,16},{8,24},{16,0},{24,8},{1,17},{9,25},{17,1},{25,9},{2,18},{10... | collective-permute-start | bytes 786440 | tf_op jit(solution)/shard_map/ppermute | solution.py:308
  52.4 0.7 %copy-start = (bf16[128,1024]{1,0:T(8,128)(2,1)}, bf16[128,1024]{1,0:T(8,128)(2,1)S(1)}, u32[]{:S(2)}) copy-start(bf16[128,1024]{1,0:T(8,128)(2,1)S(1)} %collective-permute-done.4.a_ref) | copy-start | bytes 786436
  52.4 0.8 %copy-start.1 = (bf16[128,1024]{1,0:T(8,128)(2,1)}, bf16[128,1024]{1,0:T(8,128)(2,1)S(1)}, u32[]{:S(2)}) copy-start(bf16[128,1024]{1,0:T(8,128)(2,1)S(1)} %collective-permute-done.5.b_ref) | copy-start | bytes 786436
